TPU v7x, 32 devices: a whole 2x2x4 slice. The times are simulated.
32 devices in a mesh: dp: 16 (over z, x, core), ctx: 2 (over y).
Axes of the slice: x: 2, y: 2, z: 4, core: 2. Of those that a mesh axis runs over, the one named last changes fastest.
Arguments:
- tokens_in: bfloat16 [16, 768, 1152], P('dp', 'ctx'), may hold values from -6 to 6
- cotangent: float32 [16, 768, 1152], P('dp', 'ctx'), may hold values from -6 to 6
- token_mask: int32 [16, 768], P('dp', 'ctx'), may hold values from 0 to 1, as said below
- attn_params: float32 [1152, 4613], P(('dp', 'ctx'))
- attn_first: float32 [1152, 4613], P(('dp', 'ctx')), may hold values from -60 to 60
- attn_second: float32 [1152, 4613], P(('dp', 'ctx')), may hold values from 1 to 100
- feed_params: float32 [1152, 8611], P(('dp', 'ctx'))
- feed_first: float32 [1152, 8611], P(('dp', 'ctx')), may hold values from -60 to 60
- feed_second: float32 [1152, 8611], P(('dp', 'ctx')), may hold values from 1 to 100
- up_bias: float32 [4304], replicated, may hold values from -3 to 3
- up_bias_first: float32 [4304], replicated, may hold values from -60 to 60
- up_bias_second: float32 [4304], replicated, may hold values from 1 to 100
Outputs:
- block_out: float32 [16, 768, 1152], P('dp', 'ctx')
- grad_input: float32 [16, 768, 1152], P('dp', 'ctx')
- grad_attn: float32 [1152, 4613], P(('dp', 'ctx'))
- grad_feed: float32 [1152, 8611], P(('dp', 'ctx'))
- grad_up_bias: float32 [4304], replicated
- new_attn: float32 [1152, 4613], P(('dp', 'ctx'))
- new_attn_first: float32 [1152, 4613], P(('dp', 'ctx'))
- new_attn_second: float32 [1152, 4613], P(('dp', 'ctx'))
- new_feed: float32 [1152, 8611], P(('dp', 'ctx'))
- new_feed_first: float32 [1152, 8611], P(('dp', 'ctx'))
- new_feed_second: float32 [1152, 8611], P(('dp', 'ctx'))
- new_up_bias: float32 [4304], replicated
- new_up_bias_first: float32 [4304], replicated
- new_up_bias_second: float32 [4304], replicated
Inputs may be any that keep to these rules, and one draw needn't show every extreme that they name: `token_mask`: each image has exactly 729 valid tokens, at positions drawn for each image.
All inputs are finite; a program needn't handle non-finite values.
Results may differ from a plain program's by a relative error of at most 0.012.
Values may be sent and summed in bfloat16 or wider, within the bound.
No kernel may reach another device: no remote copies, remote signals or barrier semaphores. Data moves between devices by JAX's collectives and lax.ppermute only.
A program may use at most 320 MiB of HBM per device.

v0:
```python
import math

import jax
import jax.numpy as jnp
from jax import lax
from jax.sharding import PartitionSpec as P


HD = 72
STEP = 4


eps_norm = 1e-06
lr_rate = 0.01
beta_one = 0.9
beta_two = 0.999
eps_adam = 1e-08
decay_rate = 0.05

bf16 = jnp.bfloat16
f32 = jnp.float32


def gelu_tanh(values):
    return jax.nn.gelu(values, approximate=True)


def norm_stats(values):
    mean_val = jnp.mean(values, axis=-1, keepdims=True)
    centred = values - mean_val
    var_val = jnp.mean(centred * centred, axis=-1, keepdims=True)
    inv_std = lax.rsqrt(var_val + eps_norm)
    return centred * inv_std, inv_std


def norm_backward(grad_out, normed, inv_std, gain):
    scaled = grad_out * gain
    return inv_std * (
        scaled
        - jnp.mean(scaled, axis=-1, keepdims=True)
        - normed * jnp.mean(scaled * normed, axis=-1, keepdims=True)
    )


def adamw_step(param, first, second, grad):
    first_new = beta_one * first + (1.0 - beta_one) * grad
    second_new = beta_two * second + (1.0 - beta_two) * grad * grad
    first_hat = first_new / (1.0 - beta_one**STEP)
    second_hat = second_new / (1.0 - beta_two**STEP)
    param_new = param - lr_rate * (
        first_hat / (jnp.sqrt(second_hat) + eps_adam) + decay_rate * param
    )
    return (param_new, first_new, second_new)


def mm(left, right):
    return jnp.dot(left, right, preferred_element_type=f32)


def mm_nt(left, right):
    return lax.dot_general(left, right, (((1,), (1,)), ((), ())), preferred_element_type=f32)


def mm_tn(left, right):
    return lax.dot_general(left, right, (((0,), (0,)), ((), ())), preferred_element_type=f32)


def dp_swap(value, mask):
    count = lax.axis_size("dp")
    return lax.ppermute(value, "dp", [(i, i ^ mask) for i in range(count)])


def core_swap(value):
    return dp_swap(value, 1)


def x_swap(value):
    return dp_swap(value, 2)


def z_swap(value, step):
    return dp_swap(value, 4 * step)


def y_swap(value):
    count = lax.axis_size("ctx")
    return lax.ppermute(value, "ctx", [(i, i ^ 1) for i in range(count)])


def after(value, *others):
    return lax.optimization_barrier((value, others))[0]


def gather_line(block, depth):
    return [block] + [z_swap(block, step) for step in range(1, depth)]


def gather_sides(line, *others):
    whole = after(jnp.concatenate(line, axis=0), *others)
    return whole, x_swap(whole), y_swap(whole)


def gather_corner(sides, *others):
    whole, over_x, over_y = sides
    half = whole.shape[0] // 2
    send_x, send_y = after((over_x[:half], over_y[half:]), *others)
    return [whole, over_x, over_y, y_swap(send_x), x_swap(send_y)]


def gather_all(pieces):
    return jnp.concatenate(pieces, axis=0)


def add_half(left, right):
    return (left.astype(f32) + right.astype(f32)).astype(bf16)


def scatter_corner(corner, cut):
    split = corner.shape[0] * cut // 2
    from_y = y_swap(corner[:split]) if cut > 0 else None
    from_x = x_swap(corner[split:]) if cut < 2 else None
    return from_y, from_x


def scatter_sides(chunks, corners, *others):
    near, side_x, side_y = chunks
    from_y, from_x = after(corners, *others)
    if from_y is not None:
        split = from_y.shape[0]
        side_x = jnp.concatenate([add_half(side_x[:split], from_y), side_x[split:]], axis=0)
    if from_x is not None:
        split = near.shape[0] - from_x.shape[0]
        side_y = jnp.concatenate([side_y[:split], add_half(side_y[split:], from_x)], axis=0)
    return near, x_swap(side_x), y_swap(side_y)


def scatter_line(sides, depth, *others):
    near, got_x, got_y = after(sides, *others)
    total = (near.astype(f32) + got_x.astype(f32) + got_y.astype(f32)).astype(bf16)
    rows = total.shape[0] // depth
    parts = [total[step * rows : (step + 1) * rows] for step in range(depth)]
    return parts[:1] + [z_swap(parts[step], step) for step in range(1, depth)]


def scatter_done(parts, *others):
    parts = after(parts, *others)
    out = parts[0].astype(f32)
    for part in parts[1:]:
        out = out + part.astype(f32)
    return out


def weight_chunks(left, right):
    size = left.shape[1] // 4
    return [mm_tn(left[:, i * size : (i + 1) * size], right).astype(bf16) for i in range(3)]


def weight_corner(left, right):
    size = left.shape[1] // 4
    return mm_tn(left[:, 3 * size :], right).astype(bf16)


def split_two(values):
    high = lax.reduce_precision(values, 8, 7)
    return jnp.concatenate([high.astype(bf16), (values - high).astype(bf16)], axis=1)


def head_scores(query_heads, key_heads, valid):
    raw = jnp.einsum("bqhd,bkhd->bhqk", query_heads, key_heads, preferred_element_type=f32)
    raw = raw * (1.0 / math.sqrt(HD))
    return jnp.where(valid[:, None, None, :], raw, -1e30)


def attend(query, key, value, valid):
    images, rows, width = query.shape
    heads = width // HD
    q_heads = query.reshape(images, rows, heads, HD)
    k_heads = key.reshape(images, -1, heads, HD)
    v_heads = value.reshape(images, -1, heads, HD)
    scores = head_scores(q_heads, k_heads, valid)
    row_max = jnp.max(scores, axis=-1, keepdims=True)
    log_total = row_max + jnp.log(jnp.sum(jnp.exp(scores - row_max), axis=-1, keepdims=True))
    prob = jnp.exp(scores - log_total).astype(bf16)
    mixed = jnp.einsum("bhqk,bkhd->bqhd", prob, v_heads, preferred_element_type=f32)
    return mixed.reshape(images, rows, width).astype(bf16), log_total


def attend_back(query, key, value, valid, mixed, log_total, grad_mixed):
    images, rows, width = query.shape
    heads = width // HD
    keys = key.shape[1]
    q_heads = query.reshape(images, rows, heads, HD)
    k_heads = key.reshape(images, keys, heads, HD)
    v_heads = value.reshape(images, keys, heads, HD)
    g_heads = grad_mixed.reshape(images, rows, heads, HD)
    o_heads = mixed.reshape(images, rows, heads, HD)
    scores = head_scores(q_heads, k_heads, valid)
    prob = jnp.exp(scores - log_total)
    prob_half = prob.astype(bf16)
    grad_prob = jnp.einsum("bqhd,bkhd->bhqk", g_heads, v_heads, preferred_element_type=f32)
    delta = jnp.einsum("bqhd,bqhd->bhq", g_heads.astype(f32), o_heads.astype(f32))[..., None]
    grad_score = (prob * (grad_prob - delta)).astype(bf16)
    scale = 1.0 / math.sqrt(HD)
    grad_q = jnp.einsum("bhqk,bkhd->bqhd", grad_score, k_heads, preferred_element_type=f32)
    grad_k = jnp.einsum("bhqk,bqhd->bkhd", grad_score, q_heads, preferred_element_type=f32)
    grad_v = jnp.einsum("bhqk,bqhd->bkhd", prob_half, g_heads, preferred_element_type=f32)
    return (
        grad_q.reshape(images, rows, width) * scale,
        grad_k.reshape(images, keys, width) * scale,
        grad_v.reshape(images, keys, width),
        grad_score,
    )


def body(
    tokens_in,
    cotangent,
    token_mask,
    attn_params,
    attn_first,
    attn_second,
    feed_params,
    feed_first,
    feed_second,
    up_bias,
    up_bias_first,
    up_bias_second,
):
    images, local_len, width = tokens_in.shape
    hidden = up_bias.shape[0]
    owned = attn_params.shape[0]
    dp_count = lax.axis_size("dp")
    ctx_count = lax.axis_size("ctx")
    assert images == 1 and ctx_count == 2 and dp_count % 4 == 0
    depth = dp_count // 4
    dp_at = lax.axis_index("dp")
    y_at = lax.axis_index("ctx")
    core = dp_at % 2
    x_at = (dp_at // 2) % 2
    z_at = dp_at // 4
    first_core = core == 0
    half_w = width // 2
    half_h = hidden // 2

    rows_own = tokens_in[0]
    mask_own = token_mask.astype(f32)
    mask_img = jnp.concatenate([mask_own, y_swap(mask_own)], axis=1)
    mask_all = jnp.concatenate([mask_img, core_swap(mask_img)], axis=0)
    valid = mask_all > 0

    attn_half = attn_params.astype(bf16)
    feed_half = feed_params.astype(bf16)

    def pick(at):
        parts = [
            attn_half[:, i * width + at * half_w : i * width + (at + 1) * half_w]
            for i in range(4)
        ]
        parts.append(attn_half[:, 4 * width :])
        parts.append(feed_half[:, 2 * hidden :])
        for i in range(2):
            parts.append(feed_half[:, i * hidden + at * half_h : i * hidden + (at + 1) * half_h])
        return jnp.concatenate(parts, axis=1)

    part_zero, part_one = pick(0), pick(1)
    keep = jnp.where(first_core, part_zero, part_one)
    give = jnp.where(first_core, part_one, part_zero)
    got = core_swap(give)
    shard = jnp.concatenate(
        [jnp.where(first_core, keep, got), jnp.where(first_core, got, keep)], axis=0
    )
    vecs = attn_params.shape[1] - 4 * width + feed_params.shape[1] - 2 * hidden
    cut = 4 * half_w + vecs
    line_a = gather_line(shard[:, :cut], depth)
    sides_a = gather_sides(line_a)
    all_a = gather_corner(sides_a)
    w_attn = gather_all(all_a)
    line_c = gather_line(after(shard[:, cut : cut + half_h], *sides_a[1:]), depth)
    rows_far = y_swap(after(rows_own, shard))

    block = 2 * owned
    spot = after(jnp.arange(width, dtype=jnp.int32), shard)
    place = spot // block
    y_of = y_at ^ (place // (2 * depth))
    x_of = x_at ^ ((place // depth) % 2)
    z_of = z_at ^ (place % depth)
    core_of = (spot % block) // owned
    natural = (((z_of * 2 + x_of) * 2 + core_of) * 2 + y_of) * owned + spot % owned
    row_ids = lax.broadcasted_iota(jnp.int32, (2 * width, width), 0) % width
    order_two = (row_ids == natural[None, :]).astype(bf16)
    order = order_two[:width]

    def to_local(values):
        return mm(split_two(values), order_two)

    order_back = jnp.tile(order.T, (2, 1))

    def to_natural(values):
        return mm(split_two(values), order_back)

    w_q, w_k, w_v, w_o = (w_attn[:, i * half_w : (i + 1) * half_w] for i in range(4))
    vec = w_attn[:, 4 * half_w :]
    vec_nat = mm(order, vec[:, 2:4])
    vec_t = vec.astype(f32).T
    gain_one, shift_one, bias_o = vec_t[0], vec_t[1], vec_t[4]
    gain_two, shift_two, bias_d = vec_t[5], vec_t[6], vec_t[7]
    bias_qv = jnp.where(first_core, vec_nat[:half_w], vec_nat[half_w:]).T
    bias_up = lax.optimization_barrier(up_bias.astype(bf16)).astype(f32)
    bias_up = jnp.where(first_core, bias_up[:half_h], bias_up[half_h:])

    live = mask_own.reshape(local_len, 1)
    grad_rows = to_local(after(cotangent[0], sides_a[0]) * live)
    grad_half = grad_rows.astype(bf16)
    grad_both = jnp.concatenate([grad_half, core_swap(grad_half)], axis=0)

    rows_img = mm(after(jnp.concatenate([rows_own, rows_far], axis=0), sides_a[0]), order)
    rows_in = rows_img[:local_len]
    norm_img, scale_img = norm_stats(rows_img)
    half_img = (norm_img * gain_one + shift_one).astype(bf16)
    half_far = core_swap(half_img)
    one_all = jnp.concatenate([half_img, half_far], axis=0)
    one_own = jnp.concatenate([half_img[:local_len], half_far[:local_len]], axis=0)
    seq = 2 * local_len
    query = (mm(one_own, w_q) + bias_qv[0]).astype(bf16).reshape(2, local_len, half_w)
    key = mm(one_all, w_k).astype(bf16).reshape(2, seq, half_w)
    value = (mm(one_all, w_v) + bias_qv[1]).astype(bf16).reshape(2, seq, half_w)
    sides_c = gather_sides(line_c, query, key, value)
    line_d = gather_line(after(shard[:, cut + half_h :], *line_c), depth)
    query, key, value = after((query, key, value), sides_c[0])
    mixed, log_total = attend(query, key, value, valid)
    sides_d = gather_sides(line_d, mixed)
    all_c = gather_corner(sides_c, mixed)
    w_up = gather_all(all_c)
    mixed = after(mixed, sides_d[0], *all_c[1:3])
    mixed_rows = mixed.reshape(2 * local_len, half_w)
    part = mm_nt(mixed_rows, w_o)
    resid = rows_in + part[:local_len] + core_swap(part[local_len:]) + bias_o

    norm_two, scale_two = norm_stats(resid)
    half_two = (norm_two * gain_two + shift_two).astype(bf16)
    all_d = gather_corner(sides_d, half_two)
    w_down = gather_all(all_d)
    two_both = jnp.concatenate([half_two, core_swap(half_two)], axis=0)
    pre_act = mm(two_both, w_up) + bias_up
    act_half = gelu_tanh(pre_act).astype(bf16)
    down_corner = scatter_corner(weight_corner(grad_both, act_half), 2)
    down_chunks = weight_chunks(grad_both, act_half)
    grad_act = mm(after(grad_both, *down_chunks), w_down)
    grad_pre = jax.vjp(gelu_tanh, pre_act)[1](grad_act)[0]
    grad_pre_half = grad_pre.astype(bf16)
    up_corner = scatter_corner(weight_corner(two_both, grad_pre_half), 0)
    part = mm_nt(grad_pre_half, w_up)
    part_far = core_swap(part[local_len:])
    up_chunks = weight_chunks(two_both, after(grad_pre_half, part))
    down_sides = scatter_sides(down_chunks, down_corner, part)
    grad_norm_two = part[:local_len] + after(part_far, up_chunks)
    grad_resid = grad_rows + norm_backward(grad_norm_two, norm_two, scale_two, gain_two)
    grad_resid_half = grad_resid.astype(bf16)
    resid_far = core_swap(grad_resid_half)
    up_sides = scatter_sides(up_chunks, up_corner, grad_resid_half)
    resid_both = jnp.concatenate([grad_resid_half, resid_far], axis=0)

    grad_mixed = mm(resid_both, w_o).astype(bf16).reshape(2, local_len, half_w)
    grad_q, grad_k, grad_v, grad_score = attend_back(
        query, key, value, valid, mixed, log_total, grad_mixed
    )
    down_line = scatter_line(down_sides, depth, grad_score)
    grad_q = grad_q.reshape(2 * local_len, half_w)
    grad_k = grad_k.reshape(2 * seq, half_w)
    grad_v = grad_v.reshape(2 * seq, half_w)
    grad_q_half = grad_q.astype(bf16)
    grad_k_half = grad_k.astype(bf16)
    grad_v_half = grad_v.astype(bf16)
    corner_all = jnp.concatenate(
        [
            weight_corner(one_own, grad_q_half),
            weight_corner(one_all, grad_k_half),
            weight_corner(one_all, grad_v_half),
            weight_corner(resid_both, mixed_rows),
        ],
        axis=1,
    )
    attn_corner = scatter_corner(corner_all, 1)
    up_line = scatter_line(up_sides, depth, corner_all)
    pieces = [
        weight_chunks(one_own, grad_q_half),
        weight_chunks(one_all, grad_k_half),
        weight_chunks(one_all, grad_v_half),
        weight_chunks(resid_both, mixed_rows),
    ]
    attn_chunks = [jnp.concatenate([piece[i] for piece in pieces], axis=1) for i in range(3)]
    attn_sides = scatter_sides(attn_chunks, attn_corner)
    grad_q_half, grad_k_half, grad_v_half = after(
        (grad_q_half, grad_k_half, grad_v_half), attn_chunks
    )
    part_q = mm_nt(grad_q_half, w_q).reshape(2, local_len, width)
    part_kv = (mm_nt(grad_k_half, w_k) + mm_nt(grad_v_half, w_v)).reshape(2, seq, width)
    part_own = jnp.concatenate([part_q[0] + part_kv[0, :local_len], part_kv[0, local_len:]], axis=0)
    part_sib = jnp.concatenate([part_q[1] + part_kv[1, :local_len], part_kv[1, local_len:]], axis=0)
    part_img = part_own + core_swap(part_sib)
    part_far = part_img[local_len:].astype(bf16)
    part_far = y_swap(jnp.concatenate([part_far[:, half_w:], part_far[:, :half_w]], axis=1))
    grad_norm_one = part_img[:local_len] + part_far.astype(f32)
    grad_in = grad_resid + norm_backward(
        grad_norm_one, norm_img[:local_len], scale_img[:local_len], gain_one
    )
    grad_input = to_natural(grad_in)[None]

    zeros = jnp.zeros((half_w,), f32)
    sum_q = jnp.sum(grad_q, axis=0)
    sum_v = jnp.sum(grad_v, axis=0)

    def spread(vector):
        return jnp.where(
            first_core,
            jnp.concatenate([vector, zeros]),
            jnp.concatenate([zeros, vector]),
        )

    cols = jnp.stack(
        [
            jnp.sum(part_img * norm_img, axis=0),
            jnp.sum(part_img, axis=0),
            jnp.sum(grad_resid, axis=0),
            jnp.sum(grad_norm_two * norm_two, axis=0),
            jnp.sum(grad_norm_two, axis=0),
            jnp.sum(grad_rows, axis=0),
        ],
        axis=0,
    )
    cols = to_natural(cols).reshape(1, -1)
    bias_sum = jnp.sum(grad_pre, axis=0, keepdims=True)
    sums = jnp.concatenate(
        [cols, spread(sum_q)[None], spread(sum_v)[None], bias_sum], axis=1
    )
    sums = sums + y_swap(sums)
    mask = 2
    while mask < dp_count:
        sums = sums + dp_swap(sums, mask)
        mask *= 2
    sums_far = core_swap(sums)
    cols = (sums + sums_far)[0, : 8 * width].reshape(8, width)
    bias_mine, bias_far = sums[:, 8 * width :], sums_far[:, 8 * width :]

    down_sum = scatter_done(down_line, part_img)
    up_sum = scatter_done(up_line, part_img)
    attn_line = scatter_line(attn_sides, depth, part_img)
    attn_sum = scatter_done(attn_line)

    part_out = mm_nt(after(act_half, *attn_chunks), w_down)
    block_rows = resid + part_out[:local_len] + core_swap(part_out[local_len:]) + bias_d
    block_out = to_natural(block_rows)[None]

    def trade(values):
        upper, lower = values[:owned], values[owned:]
        mine = jnp.where(first_core, upper, lower)
        other = core_swap(jnp.where(first_core, lower, upper))
        return mine, other

    def join(mine, other):
        return jnp.where(
            first_core,
            jnp.concatenate([mine, other], axis=1),
            jnp.concatenate([other, mine], axis=1),
        )

    down_mine, down_other = trade(down_sum)
    up_mine, up_other = trade(up_sum)
    attn_mine, attn_other = trade(attn_sum)
    device_at = dp_at * ctx_count + y_at
    vec_sum = lax.dynamic_slice_in_dim(cols.T, device_at * owned, owned, axis=0)
    grad_attn = jnp.concatenate(
        [
            join(
                attn_mine[:, i * half_w : (i + 1) * half_w],
                attn_other[:, i * half_w : (i + 1) * half_w],
            )
            for i in range(4)
        ]
        + [vec_sum[:, :2], vec_sum[:, 6:8], vec_sum[:, 2:3]],
        axis=1,
    )
    grad_feed = jnp.concatenate(
        [join(up_mine, up_other), join(down_mine, down_other), vec_sum[:, 3:6]], axis=1
    )
    grad_up = join(bias_mine, bias_far).reshape(hidden)

    new_attn, new_attn_first, new_attn_second = adamw_step(
        attn_params, attn_first, attn_second, grad_attn
    )
    new_feed, new_feed_first, new_feed_second = adamw_step(
        feed_params, feed_first, feed_second, grad_feed
    )
    new_up, new_up_first, new_up_second = adamw_step(
        up_bias, up_bias_first, up_bias_second, grad_up
    )
    return (
        block_out,
        grad_input,
        grad_attn,
        grad_feed,
        grad_up,
        new_attn,
        new_attn_first,
        new_attn_second,
        new_feed,
        new_feed_first,
        new_feed_second,
        new_up,
        new_up_first,
        new_up_second,
    )


def solution(mesh):
    tokens = P("dp", "ctx", None)
    params = P(("dp", "ctx"), None)

    return jax.shard_map(
        body,
        mesh=mesh,
        in_specs=(tokens, tokens, P("dp", "ctx")) + (params,) * 6 + (P(),) * 3,
        out_specs=(tokens, tokens, params, params, P()) + (params,) * 6 + (P(),) * 3,
        check_vma=False,
    )
```

profile of v0, /device:TPU:1, one launch (start us, length us, event | category | flops | bytes accessed | tf_op | source)
XLA Modules:
  0.0 636.5 jit_solution(10469755956249454846)
XLA Ops:
  27.9 10.0 %collective-permute-done.4 = bf16[72,2312]{1,0:T(8,128)(2,1)} collective-permute-done((bf16[72,2312]{1,0:T(8,128)(2,1)S(1)}, bf16[72,2312]{1,0:T(8,128)(2,1)}, u32[]{:S(2)}, u32[]{:S(2)}) %collective-permute-start.4) | collective-permute-done | bytes 332960 | tf_op jit(solution)/shard_map/ppermute | solution.py:70
  47.8 21.4 %collective-permute-done.5 = bf16[288,2312]{1,0:T(8,128)(2,1)S(1)} collective-permute-done((bf16[288,2312]{1,0:T(8,128)(2,1)S(1)}, bf16[288,2312]{1,0:T(8,128)(2,1)S(1)}, u32[]{:S(2)}, u32[]{:S(2)}) %collective-permute-start.5) | collective-permute-done | bytes 1331744 | tf_op jit(solution)/shard_map/ppermute | solution.py:70
  72.2 12.1 %collective-permute-done.7 = bf16[144,2312]{1,0:T(8,128)(2,1)S(1)} collective-permute-done((bf16[144,2312]{1,0:T(8,128)(2,1)S(1)}, bf16[144,2312]{1,0:T(8,128)(2,1)S(1)}, u32[]{:S(2)}, u32[]{:S(2)}) %collective-permute-start.7) | collective-permute-done | bytes 665888 | tf_op jit(solution)/shard_map/ppermute | solution.py:87
  94.9 8.8 %collective-permute-start.10 = (bf16[72,2152]{1,0:T(8,128)(2,1)S(1)}, bf16[72,2152]{1,0:T(8,128)(2,1)S(1)}, u32[]{:S(2)}, u32[]{:S(2)}) collective-permute-start(bf16[72,2152]{1,0:T(8,128)(2,1)S(1)} %copy-done.62), channel_id=1, source_target_pairs={{0,8},{2,10},{4,12},{6,14},{8,0},{10,2},{12,4},{14,6},{16,24},{18,... | collective-permute-start | bytes 929672 | tf_op jit(solution)/shard_map/ppermute | solution.py:70
  111.2 5.5 collective-permute-done.10
  116.6 9.4 %collective-permute-done.12 = bf16[72,2152]{1,0:T(8,128)(2,1)S(1)} collective-permute-done((bf16[72,2152]{1,0:T(8,128)(2,1)S(1)}, bf16[72,2152]{1,0:T(8,128)(2,1)S(1)}, u32[]{:S(2)}, u32[]{:S(2)}) %collective-permute-start.12) | collective-permute-done | bytes 309920 | tf_op jit(solution)/shard_map/ppermute | solution.py:70
  126.1 7.0 %collective-permute-start.15 = (bf16[72,2152]{1,0:T(8,128)(2,1)S(1)}, bf16[72,2152]{1,0:T(8,128)(2,1)S(1)}, u32[]{:S(2)}, u32[]{:S(2)}) collective-permute-start(bf16[72,2152]{1,0:T(8,128)(2,1)S(1)} %get-tuple-element.74), channel_id=1, source_target_pairs={{0,8},{2,10},{4,12},{6,14},{8,0},{10,2},{12,4},{14,6},{16,24},{18,... | collective-permute-start | bytes 929672 | tf_op jit(solution)/shard_map/ppermute | solution.py:70
  136.3 7.6 %collective-permute-done.15 = bf16[72,2152]{1,0:T(8,128)(2,1)S(1)} collective-permute-done((bf16[72,2152]{1,0:T(8,128)(2,1)S(1)}, bf16[72,2152]{1,0:T(8,128)(2,1)S(1)}, u32[]{:S(2)}, u32[]{:S(2)}) %collective-permute-start.15) | collective-permute-done | bytes 309920 | tf_op jit(solution)/shard_map/ppermute | solution.py:70
  144.7 9.6 %collective-permute-done.17 = bf16[72,2152]{1,0:T(8,128)(2,1)S(1)} collective-permute-done((bf16[72,2152]{1,0:T(8,128)(2,1)S(1)}, bf16[72,2152]{1,0:T(8,128)(2,1)S(1)}, u32[]{:S(2)}, u32[]{:S(2)}) %collective-permute-start.17) | collective-permute-done | bytes 309920 | tf_op jit(solution)/shard_map/ppermute | solution.py:70
  166.9 5.9 convolution_convert_fusion.8
  195.0 6.1 convolution_convert_fusion.9
  210.6 12.0 %collective-permute-start.20 = (f32[384,1152]{1,0:T(8,128)S(1)}, f32[384,1152]{1,0:T(8,128)S(1)}, u32[]{:S(2)}, u32[]{:S(2)}) collective-permute-start(f32[384,1152]{1,0:T(8,128)S(1)} %slice.539), channel_id=1, source_target_pairs={{0,2},{2,0},{4,6},{6,4},{8,10},{10,8},{12,14},{14,12},{16,18},{18,... | collective-permute-start | bytes 5308424 | tf_op jit(solution)/shard_map/ppermute | solution.py:70
  239.7 6.1 collective-permute-done.22
  245.9 12.8 %collective-permute-start.21 = (bf16[384,1152]{1,0:T(8,128)(2,1)S(1)}, bf16[384,1152]{1,0:T(8,128)(2,1)S(1)}, u32[]{:S(2)}, u32[]{:S(2)}) collective-permute-start(bf16[384,1152]{1,0:T(8,128)(2,1)S(1)} %add_convert_fusion.7), channel_id=1, source_target_pairs={{0,2},{2,0},{4,6},{6,4},{8,10},{10,8},{12,14},{14,12},{16,18},{18,... | collective-permute-start | bytes 2654216 | tf_op jit(solution)/shard_map/ppermute | solution.py:70
  260.0 14.3 %collective-permute-done.28 = bf16[144,2152]{1,0:T(8,128)(2,1)S(1)} collective-permute-done((bf16[144,2152]{1,0:T(8,128)(2,1)S(1)}, bf16[144,2152]{1,0:T(8,128)(2,1)S(1)}, u32[]{:S(2)}, u32[]{:S(2)}) %collective-permute-start.28) | collective-permute-done | bytes 619808 | tf_op jit(solution)/shard_map/ppermute | solution.py:70
  274.4 8.8 %multiply_convert_fusion.1 = (bf16[768,2152]{0,1:T(8,128)(2,1)S(1)}, f32[768,2152]{0,1:T(8,128)}) fusion(f32[2152]{0:T(1024)S(1)} %copy-done.84, bf16[1152,2152]{1,0:T(8,128)(2,1)S(1)} %constant_dynamic-update-slice_fusion.5, bf16[384,1152]{1,0:T(8,128)(2,1)S(1)} %collective-permute-done.21, bf16[384,1152]{1,0:T(8,128)(2,1)S(1)} %add_convert_fusion.7), kind=kOutput, calls=%fused_computation.16 | convolution fusion | flops 3827970048 | bytes 16652704 | tf_op jit(solution)/shard_map/dot_general | solution.py:57
  294.8 12.6 %fusion.169 = (f32[2152]{0:T(1024)}, bf16[768,2152]{0,1:T(8,128)(2,1)S(1)}) fusion(f32[768,2152]{0,1:T(8,128)} %get-tuple-element.217, f32[2152]{0:T(1024)S(1)} %copy-done.84, bf16[768,1152]{1,0:T(8,128)(2,1)S(1)} %pad_maximum_fusion.4, bf16[1152,2152]{1,0:T(8,128)(2,1)S(1)} %constant_dynamic-update-slice_fusion.10), kind=kOutput, calls=%fused_computation.383 | convolution fusion | flops 3844261888 | bytes 16661312 | tf_op jit(solution)/shard_map/dot_general | solution.py:57
  328.9 16.8 %collective-permute-done.54 = bf16[288,2152]{1,0:T(8,128)(2,1)S(1)} collective-permute-done((bf16[288,2152]{1,0:T(8,128)(2,1)S(1)}, bf16[288,2152]{1,0:T(8,128)(2,1)S(1)}, u32[]{:S(2)}, u32[]{:S(2)}) %collective-permute-start.54) | collective-permute-done | bytes 1239584 | tf_op jit(solution)/shard_map/ppermute | solution.py:87
  366.4 11.1 %bitcast_convert_fusion = (bf16[2,768,8,72]{1,3,2,0:T(8,128)(2,1)S(1)}, f32[2,8,72,768]{3,2,1,0:T(8,128)}) fusion(f32[2,8,384,768]{3,2,1,0:T(8,128)} %copy-done, f32[2,8,384]{2,1,0:T(8,128)S(1)} %copy-done.83, pred[2,768]{1,0:T(4,128)(4,1)S(1)} %maximum_compare_fusion, bf16[2,384,8,72]{1,0,3,2:T(2,128)(2,1)S(1)} %copy-done.49), kind=kOutput, calls=%fused_computation.37 | convolution fusion | flops 699236352 | bytes 25093632 | tf_op jit(solution)/shard_map/bhqk,bqhd->bkhd/dot_general | solution.py:206
  379.0 10.6 %multiply_convert_fusion = bf16[2,8,384,768]{3,2,1,0:T(8,128)(2,1)S(1)} fusion(f32[2,8,384,768]{3,2,1,0:T(8,128)} %copy-done, f32[2,8,384]{2,1,0:T(8,128)S(1)} %multiply_reduce_fusion.2, f32[2,8,384]{2,1,0:T(8,128)S(1)} %copy-done.83, pred[2,768]{1,0:T(4,128)(4,1)S(1)} %maximum_compare_fusion, bf16[2,768,8,72]{1,3,2,0:T(8,128)(2,1)S(1)} %bitcast.155, ...), kind=kOutput, calls=%fused_computation | convolution fusion | flops 707788800 | bytes 31016448 | tf_op jit(solution)/shard_map/bqhd,bkhd->bhqk/dot_general | solution.py:200
  470.9 7.0 %fusion.188 = f32[768,1152]{1,0:T(8,128)} fusion(bf16[768,2152]{0,1:T(8,128)(2,1)S(1)} %copy-done.88, bf16[1152,2152]{1,0:T(8,128)(2,1)S(1)} %bitcast.165), kind=kOutput, calls=%fused_computation.399 | convolution fusion | flops 3807903744 | bytes 11802624 | tf_op jit(solution)/shard_map/dot_general | solution.py:61
  495.5 10.5 %collective-permute-done.34 = bf16[144,2304]{1,0:T(8,128)(2,1)S(1)} collective-permute-done((bf16[144,2304]{1,0:T(8,128)(2,1)S(1)}, bf16[144,2304]{1,0:T(8,128)(2,1)S(1)}, u32[]{:S(2)}, u32[]{:S(2)}) %collective-permute-start.34) | collective-permute-done | bytes 663584 | tf_op jit(solution)/shard_map/ppermute | solution.py:87
  535.3 13.1 %collective-permute-done.51 = bf16[72,2152]{1,0:T(8,128)(2,1)} collective-permute-done((bf16[72,2152]{1,0:T(8,128)(2,1)S(1)}, bf16[72,2152]{1,0:T(8,128)(2,1)}, u32[]{:S(2)}, u32[]{:S(2)}) %collective-permute-start.51) | collective-permute-done | bytes 309920 | tf_op jit(solution)/shard_map/ppermute | solution.py:70
  572.8 13.3 %collective-permute-done.44 = f32[1,11368]{1,0:T(1,128)S(1)} collective-permute-done((f32[1,11368]{1,0:T(1,128)S(1)}, f32[1,11368]{1,0:T(1,128)S(1)}, u32[]{:S(2)}, u32[]{:S(2)}) %collective-permute-start.44) | collective-permute-done | bytes 45504 | tf_op jit(solution)/shard_map/ppermute | solution.py:70
  (514 shorter events, 381.5 us)
Async XLA Ops:
  39.3 29.9 %collective-permute-start.5 = (bf16[288,2312]{1,0:T(8,128)(2,1)S(1)}, bf16[288,2312]{1,0:T(8,128)(2,1)S(1)}, u32[]{:S(2)}, u32[]{:S(2)}) collective-permute-start(bf16[288,2312]{1,0:T(8,128)(2,1)S(1)} %pad_maximum_fusion.16), channel_id=1, source_target_pairs={{0,4},{2,6},{4,0},{6,2},{8,12},{10,14},{12,8},{14,10},{16,20},{18,... | collective-permute-start | bytes 3995144 | tf_op jit(solution)/shard_map/ppermute | solution.py:70
  40.5 29.6 %collective-permute-start.6 = (bf16[288,2312]{1,0:T(8,128)(2,1)S(1)}, bf16[288,2312]{1,0:T(8,128)(2,1)S(1)}, u32[]{:S(2)}, u32[]{:S(2)}) collective-permute-start(bf16[288,2312]{1,0:T(8,128)(2,1)S(1)} %pad_maximum_fusion.16), channel_id=1, source_target_pairs={{0,1},{1,0},{2,3},{3,2},{4,5},{5,4},{6,7},{7,6},{8,9},{9,8},{10,11... | collective-permute-start | bytes 3995144 | tf_op jit(solution)/shard_map/ppermute | solution.py:87
  89.6 67.0 %collective-permute-start.9 = (bf16[768,1152]{1,0:T(8,128)(2,1)S(1)}, bf16[768,1152]{1,0:T(8,128)(2,1)S(1)}, u32[]{:S(2)}, u32[]{:S(2)}) collective-permute-start(bf16[768,1152]{1,0:T(8,128)(2,1)S(1)} %get-tuple-element.152), channel_id=1, source_target_pairs={{0,2},{2,0},{4,6},{6,4},{8,10},{10,8},{12,14},{14,12},{16,18},{18,... | collective-permute-start | bytes 5308424 | tf_op jit(solution)/shard_map/ppermute | solution.py:70
  109.8 93.7 %collective-permute-start.24 = (bf16[384,1152]{1,0:T(8,128)(2,1)}, bf16[384,1152]{1,0:T(8,128)(2,1)}, u32[]{:S(2)}, u32[]{:S(2)}) collective-permute-start(bf16[384,1152]{1,0:T(8,128)(2,1)} %get-tuple-element.218), channel_id=1, source_target_pairs={{0,2},{2,0},{4,6},{6,4},{8,10},{10,8},{12,14},{14,12},{16,18},{18,... | collective-permute-start | bytes 2654216 | tf_op jit(solution)/shard_map/ppermute | solution.py:70
  201.1 31.3 %collective-permute-start.25 = (bf16[288,2152]{1,0:T(8,128)(2,1)}, bf16[288,2152]{1,0:T(8,128)(2,1)S(1)}, u32[]{:S(2)}, u32[]{:S(2)}) collective-permute-start(bf16[288,2152]{1,0:T(8,128)(2,1)} %pad_maximum_fusion.21), channel_id=1, source_target_pairs={{0,4},{2,6},{4,0},{6,2},{8,12},{10,14},{12,8},{14,10},{16,20},{18,... | collective-permute-start | bytes 3718664 | tf_op jit(solution)/shard_map/ppermute | solution.py:70
  202.3 30.2 %collective-permute-start.26 = (bf16[288,2152]{1,0:T(8,128)(2,1)}, bf16[288,2152]{1,0:T(8,128)(2,1)S(1)}, u32[]{:S(2)}, u32[]{:S(2)}) collective-permute-start(bf16[288,2152]{1,0:T(8,128)(2,1)} %pad_maximum_fusion.21), channel_id=1, source_target_pairs={{0,1},{1,0},{2,3},{3,2},{4,5},{5,4},{6,7},{7,6},{8,9},{9,8},{10,11... | collective-permute-start | bytes 3718664 | tf_op jit(solution)/shard_map/ppermute | solution.py:87
  226.3 33.5 %collective-permute-start.23 = (bf16[144,2152]{1,0:T(8,128)(2,1)S(1)}, bf16[144,2152]{1,0:T(8,128)(2,1)S(1)}, u32[]{:S(2)}, u32[]{:S(2)}) collective-permute-start(bf16[144,2152]{1,0:T(8,128)(2,1)S(1)} %slice.544), channel_id=1, source_target_pairs={{0,4},{2,6},{4,0},{6,2},{8,12},{10,14},{12,8},{14,10},{16,20},{18,... | collective-permute-start | bytes 1859336 | tf_op jit(solution)/shard_map/ppermute | solution.py:70
  245.9 28.5 %collective-permute-start.21 = (bf16[384,1152]{1,0:T(8,128)(2,1)S(1)}, bf16[384,1152]{1,0:T(8,128)(2,1)S(1)}, u32[]{:S(2)}, u32[]{:S(2)}) collective-permute-start(bf16[384,1152]{1,0:T(8,128)(2,1)S(1)} %add_convert_fusion.7), channel_id=1, source_target_pairs={{0,2},{2,0},{4,6},{6,4},{8,10},{10,8},{12,14},{14,12},{16,18},{18,... | collective-permute-start | bytes 2654216 | tf_op jit(solution)/shard_map/ppermute | solution.py:70
  288.0 153.7 %collective-permute-start.56 = (bf16[288,2152]{1,0:T(8,128)(2,1)}, bf16[288,2152]{1,0:T(8,128)(2,1)}, u32[]{:S(2)}, u32[]{:S(2)}) collective-permute-start(bf16[288,2152]{1,0:T(8,128)(2,1)} %convolution_convert_fusion.5), channel_id=1, source_target_pairs={{0,1},{1,0},{2,3},{3,2},{4,5},{5,4},{6,7},{7,6},{8,9},{9,8},{10,11... | collective-permute-start | bytes 3718664 | tf_op jit(solution)/shard_map/ppermute | solution.py:87
  312.4 33.3 %collective-permute-start.29 = (f32[384,1152]{1,0:T(8,128)S(1)}, f32[384,1152]{1,0:T(8,128)S(1)}, u32[]{:S(2)}, u32[]{:S(2)}) collective-permute-start(f32[384,1152]{1,0:T(8,128)S(1)} %slice.558), channel_id=1, source_target_pairs={{0,2},{2,0},{4,6},{6,4},{8,10},{10,8},{12,14},{14,12},{16,18},{18,... | collective-permute-start | bytes 5308424 | tf_op jit(solution)/shard_map/ppermute | solution.py:70
  316.3 29.4 %collective-permute-start.54 = (bf16[288,2152]{1,0:T(8,128)(2,1)S(1)}, bf16[288,2152]{1,0:T(8,128)(2,1)S(1)}, u32[]{:S(2)}, u32[]{:S(2)}) collective-permute-start(bf16[288,2152]{1,0:T(8,128)(2,1)S(1)} %convolution_convert_fusion), channel_id=1, source_target_pairs={{0,1},{1,0},{2,3},{3,2},{4,5},{5,4},{6,7},{7,6},{8,9},{9,8},{10,11... | collective-permute-start | bytes 3718664 | tf_op jit(solution)/shard_map/ppermute | solution.py:87
  319.8 31.4 %collective-permute-start.48 = (bf16[288,2152]{1,0:T(8,128)(2,1)S(1)}, bf16[288,2152]{1,0:T(8,128)(2,1)S(1)}, u32[]{:S(2)}, u32[]{:S(2)}) collective-permute-start(bf16[288,2152]{1,0:T(8,128)(2,1)S(1)} %convolution_convert_fusion.1), channel_id=1, source_target_pairs={{0,4},{2,6},{4,0},{6,2},{8,12},{10,14},{12,8},{14,10},{16,20},{18,... | collective-permute-start | bytes 3718664 | tf_op jit(solution)/shard_map/ppermute | solution.py:70
  323.9 167.1 %collective-permute-start.47 = (bf16[288,2152]{1,0:T(8,128)(2,1)}, bf16[288,2152]{1,0:T(8,128)(2,1)}, u32[]{:S(2)}, u32[]{:S(2)}) collective-permute-start(bf16[288,2152]{1,0:T(8,128)(2,1)} %convolution_convert_fusion.3), channel_id=1, source_target_pairs={{0,4},{2,6},{4,0},{6,2},{8,12},{10,14},{12,8},{14,10},{16,20},{18,... | collective-permute-start | bytes 3718664 | tf_op jit(solution)/shard_map/ppermute | solution.py:70
  349.8 91.8 %collective-permute-start.55 = (bf16[288,2152]{1,0:T(8,128)(2,1)}, bf16[288,2152]{1,0:T(8,128)(2,1)}, u32[]{:S(2)}, u32[]{:S(2)}) collective-permute-start(bf16[288,2152]{1,0:T(8,128)(2,1)} %add_convert_fusion.4), channel_id=1, source_target_pairs={{0,4},{2,6},{4,0},{6,2},{8,12},{10,14},{12,8},{14,10},{16,20},{18,... | collective-permute-start | bytes 3718664 | tf_op jit(solution)/shard_map/ppermute | solution.py:70
  352.6 138.6 %collective-permute-start.49 = (bf16[288,2152]{1,0:T(8,128)(2,1)}, bf16[288,2152]{1,0:T(8,128)(2,1)}, u32[]{:S(2)}, u32[]{:S(2)}) collective-permute-start(bf16[288,2152]{1,0:T(8,128)(2,1)} %add_convert_fusion.6), channel_id=1, source_target_pairs={{0,1},{1,0},{2,3},{3,2},{4,5},{5,4},{6,7},{7,6},{8,9},{9,8},{10,11... | collective-permute-start | bytes 3718664 | tf_op jit(solution)/shard_map/ppermute | solution.py:87
  444.9 83.2 %collective-permute-start.57 = (bf16[72,2152]{1,0:T(8,128)(2,1)}, bf16[72,2152]{1,0:T(8,128)(2,1)}, u32[]{:S(2)}, u32[]{:S(2)}) collective-permute-start(bf16[72,2152]{1,0:T(8,128)(2,1)} %get-tuple-element.175), channel_id=1, source_target_pairs={{0,8},{2,10},{4,12},{6,14},{8,0},{10,2},{12,4},{14,6},{16,24},{18,... | collective-permute-start | bytes 929672 | tf_op jit(solution)/shard_map/ppermute | solution.py:70
  449.3 80.2 %collective-permute-start.58 = (bf16[72,2152]{1,0:T(8,128)(2,1)}, bf16[72,2152]{1,0:T(8,128)(2,1)}, u32[]{:S(2)}, u32[]{:S(2)}) collective-permute-start(bf16[72,2152]{1,0:T(8,128)(2,1)} %get-tuple-element.174), channel_id=1, source_target_pairs={{0,16},{2,18},{4,20},{6,22},{8,24},{10,26},{12,28},{14,30},{16,0},... | collective-permute-start | bytes 929672 | tf_op jit(solution)/shard_map/ppermute | solution.py:70
  450.3 79.5 %collective-permute-start.59 = (bf16[72,2152]{1,0:T(8,128)(2,1)}, bf16[72,2152]{1,0:T(8,128)(2,1)}, u32[]{:S(2)}, u32[]{:S(2)}) collective-permute-start(bf16[72,2152]{1,0:T(8,128)(2,1)} %get-tuple-element.173), channel_id=1, source_target_pairs={{0,24},{2,26},{4,28},{6,30},{8,16},{10,18},{12,20},{14,22},{16,8},... | collective-permute-start | bytes 929672 | tf_op jit(solution)/shard_map/ppermute | solution.py:70
  529.5 30.0 %collective-permute-start.37 = (bf16[288,2304]{1,0:T(8,128)(2,1)}, bf16[288,2304]{1,0:T(8,128)(2,1)}, u32[]{:S(2)}, u32[]{:S(2)}) collective-permute-start(bf16[288,2304]{1,0:T(8,128)(2,1)} %pad_maximum_fusion.18), channel_id=1, source_target_pairs={{0,1},{1,0},{2,3},{3,2},{4,5},{5,4},{6,7},{7,6},{8,9},{9,8},{10,11... | collective-permute-start | bytes 3981320 | tf_op jit(solution)/shard_map/ppermute | solution.py:87
  529.8 29.8 %collective-permute-start.36 = (bf16[288,2304]{1,0:T(8,128)(2,1)}, bf16[288,2304]{1,0:T(8,128)(2,1)}, u32[]{:S(2)}, u32[]{:S(2)}) collective-permute-start(bf16[288,2304]{1,0:T(8,128)(2,1)} %pad_maximum_fusion.17), channel_id=1, source_target_pairs={{0,4},{2,6},{4,0},{6,2},{8,12},{10,14},{12,8},{14,10},{16,20},{18,... | collective-permute-start | bytes 3981320 | tf_op jit(solution)/shard_map/ppermute | solution.py:70
  533.7 71.0 %collective-permute-start.60 = (f32[36,2152]{1,0:T(8,128)}, f32[36,2152]{1,0:T(8,128)}, u32[]{:S(2)}, u32[]{:S(2)}) collective-permute-start(f32[36,2152]{1,0:T(8,128)} %get-tuple-element.190), channel_id=1, source_target_pairs={{0,2},{2,0},{4,6},{6,4},{8,10},{10,8},{12,14},{14,12},{16,18},{18,... | collective-permute-start | bytes 929672 | tf_op jit(solution)/shard_map/ppermute | solution.py:70
  564.0 44.3 %collective-permute-start.53 = (f32[36,2152]{1,0:T(8,128)}, f32[36,2152]{1,0:T(8,128)}, u32[]{:S(2)}, u32[]{:S(2)}) collective-permute-start(f32[36,2152]{1,0:T(8,128)} %get-tuple-element.192), channel_id=1, source_target_pairs={{0,2},{2,0},{4,6},{6,4},{8,10},{10,8},{12,14},{14,12},{16,18},{18,... | collective-permute-start | bytes 929672 | tf_op jit(solution)/shard_map/ppermute | solution.py:70
  567.9 45.4 %collective-permute-start.38 = (bf16[72,2304]{1,0:T(8,128)(2,1)}, bf16[72,2304]{1,0:T(8,128)(2,1)}, u32[]{:S(2)}, u32[]{:S(2)}) collective-permute-start(bf16[72,2304]{1,0:T(8,128)(2,1)} %get-tuple-element.169), channel_id=1, source_target_pairs={{0,8},{2,10},{4,12},{6,14},{8,0},{10,2},{12,4},{14,6},{16,24},{18,... | collective-permute-start | bytes 995336 | tf_op jit(solution)/shard_map/ppermute | solution.py:70
  570.1 43.2 %collective-permute-start.39 = (bf16[72,2304]{1,0:T(8,128)(2,1)}, bf16[72,2304]{1,0:T(8,128)(2,1)}, u32[]{:S(2)}, u32[]{:S(2)}) collective-permute-start(bf16[72,2304]{1,0:T(8,128)(2,1)} %get-tuple-element.168), channel_id=1, source_target_pairs={{0,16},{2,18},{4,20},{6,22},{8,24},{10,26},{12,28},{14,30},{16,0},... | collective-permute-start | bytes 995336 | tf_op jit(solution)/shard_map/ppermute | solution.py:70
  (133 other events, 1306.4 us)
where the time goes:
time: 643 us; the launch traced here: 636 us
  matrix products  179 us (28%)
  waiting for transfers between devices  170 us (26%)
  starting transfers between devices  111 us (17%)
  local copies, waits for them, and re-layouts  97.6 us (15%)
  other arithmetic  76.9 us (12%)
    ppermute x46, waiting for transfers between devices, dp_swap(): return lax.ppermute(value, 'dp', [(i, i ^ mask) for i in range(count)])  120 us
    ppermute x46, starting transfers between devices, dp_swap(): return lax.ppermute(value, 'dp', [(i, i ^ mask) for i in range(count)])  96.5 us
    dot_general x12, matrix products, mm(): return jnp.dot(left, right, preferred_element_type=f32)  57.4 us
    dot_general x24, matrix products, mm_tn(): lax.dot_general(left, right, (((0,), (0,)), ((), ())), preferred_element_...  56.1 us
    ppermute x15, waiting for transfers between devices, y_swap(): return lax.ppermute(value, 'ctx', [(i, i ^ 1) for i in range(count)])  50.5 us
    dot_general x6, matrix products, mm_nt(): lax.dot_general(left, right, (((1,), (1,)), ((), ())), preferred_element_...  28.9 us
    unnamed x206, local copies, waits for them, and re-layouts  23.7 us
    ppermute x15, starting transfers between devices, y_swap(): return lax.ppermute(value, 'ctx', [(i, i ^ 1) for i in range(count)])  14 us
  transfers between devices with their start and end apart: 61, of which 24 were waited for; matrix products, arithmetic and copies ran while one was open for 48% of the time, Pallas kernels for 0%

commit v1 on v0

--- a/solution.py
+++ b/solution.py
@@ -3,6 +3,8 @@
 import jax
 import jax.numpy as jnp
 from jax import lax
+from jax.experimental import pallas as pl
+from jax.experimental.pallas import tpu as pltpu
 from jax.sharding import PartitionSpec as P
 
 
@@ -162,54 +164,89 @@
 
 def split_two(values):
     high = lax.reduce_precision(values, 8, 7)
-    return jnp.concatenate([high.astype(bf16), (values - high).astype(bf16)], axis=1)
-
-
-def head_scores(query_heads, key_heads, valid):
-    raw = jnp.einsum("bqhd,bkhd->bhqk", query_heads, key_heads, preferred_element_type=f32)
-    raw = raw * (1.0 / math.sqrt(HD))
-    return jnp.where(valid[:, None, None, :], raw, -1e30)
-
-
-def attend(query, key, value, valid):
-    images, rows, width = query.shape
+    return jnp.concatenate([high.astype(bf16), (values - high).astype(bf16)], axis=0)
+
+
+def attend_kernel(packed_ref, valid_ref, mixed_ref, log_ref):
+    rows, width = mixed_ref.shape[1:]
+    live = valid_ref[0] > 0
+    for head in range(width // HD):
+        at = head * HD
+        query = packed_ref[0, :rows, at : at + HD]
+        key = packed_ref[0, :, width + at : width + at + HD]
+        value = packed_ref[0, :, 2 * width + at : 2 * width + at + HD]
+        scores = mm_nt(key, query) * (1.0 / math.sqrt(HD))
+        scores = jnp.where(live, scores, -1e30)
+        top = jnp.max(scores, axis=0, keepdims=True)
+        prob = jnp.exp(scores - top)
+        total = jnp.sum(prob, axis=0, keepdims=True)
+        log_ref[0, head : head + 1, :] = top + jnp.log(total)
+        half = (prob * (1.0 / total)).astype(bf16)
+        mixed_ref[0, :, at : at + HD] = mm_tn(half, value).astype(bf16)
+
+
+def attend(packed, valid, rows, width):
+    images, seq, wide = packed.shape
     heads = width // HD
-    q_heads = query.reshape(images, rows, heads, HD)
-    k_heads = key.reshape(images, -1, heads, HD)
-    v_heads = value.reshape(images, -1, heads, HD)
-    scores = head_scores(q_heads, k_heads, valid)
-    row_max = jnp.max(scores, axis=-1, keepdims=True)
-    log_total = row_max + jnp.log(jnp.sum(jnp.exp(scores - row_max), axis=-1, keepdims=True))
-    prob = jnp.exp(scores - log_total).astype(bf16)
-    mixed = jnp.einsum("bhqk,bkhd->bqhd", prob, v_heads, preferred_element_type=f32)
-    return mixed.reshape(images, rows, width).astype(bf16), log_total
-
-
-def attend_back(query, key, value, valid, mixed, log_total, grad_mixed):
-    images, rows, width = query.shape
+    return pl.pallas_call(
+        attend_kernel,
+        grid=(images,),
+        in_specs=[pl.BlockSpec((1, seq, wide), lambda i: (i, 0, 0)), pl.BlockSpec((1, seq, 1), lambda i: (i, 0, 0))],
+        out_specs=[pl.BlockSpec((1, rows, width), lambda i: (i, 0, 0)), pl.BlockSpec((1, heads, rows), lambda i: (i, 0, 0))],
+        out_shape=[jax.ShapeDtypeStruct((images, rows, width), bf16), jax.ShapeDtypeStruct((images, heads, rows), f32)],
+        compiler_params=pltpu.CompilerParams(vmem_limit_bytes=56 << 20),
+        cost_estimate=pl.CostEstimate(flops=4*images*rows*seq*width, bytes_accessed=packed.size*2, transcendentals=images*heads*rows*seq),
+    )(packed, valid)
+
+
+def back_kernel(packed_ref, valid_ref, mixed_ref, log_ref, grad_ref, out_ref, sum_ref):
+    rows, width = mixed_ref.shape[1:]
+    seq, wide = out_ref.shape[1:]
+    scale = 1.0 / math.sqrt(HD)
+    live = valid_ref[0] > 0
+    out_ref[0, rows:, :width] = jnp.zeros((seq - rows, width), bf16)
+    if wide > 3 * width:
+        out_ref[0, :, 3 * width :] = jnp.zeros((seq, wide - 3 * width), bf16)
+    sum_ref[0] = jnp.zeros(sum_ref.shape[1:], f32)
+    for head in range(width // HD):
+        at = head * HD
+        query = packed_ref[0, :rows, at : at + HD]
+        key = packed_ref[0, :, width + at : width + at + HD]
+        value = packed_ref[0, :, 2 * width + at : 2 * width + at + HD]
+        grad = grad_ref[0, :, at : at + HD]
+        mixed = mixed_ref[0, :, at : at + HD]
+        delta = jnp.sum((grad.astype(f32) * mixed.astype(f32)).T, axis=0, keepdims=True)
+        scores = mm_nt(key, query) * scale
+        scores = jnp.where(live, scores, -1e30)
+        prob = jnp.exp(scores - log_ref[0, head : head + 1, :])
+        grad_v = mm(prob.astype(bf16), grad)
+        grad_s = (prob * (mm_nt(value, grad) - delta)).astype(bf16)
+        grad_k = mm(grad_s, query) * scale
+        grad_q = mm_tn(grad_s, key) * scale
+        out_ref[0, :rows, at : at + HD] = grad_q.astype(bf16)
+        out_ref[0, :, width + at : width + at + HD] = grad_k.astype(bf16)
+        out_ref[0, :, 2 * width + at : 2 * width + at + HD] = grad_v.astype(bf16)
+        sum_ref[0, :1, at : at + HD] = jnp.sum(grad_q, axis=0, keepdims=True)
+        sum_ref[0, :1, 2 * width + at : 2 * width + at + HD] = jnp.sum(grad_v, axis=0, keepdims=True)
+
+
+def attend_back(packed, valid, mixed, log_total, grad):
+    images, seq, wide = packed.shape
+    rows, width = mixed.shape[1:]
     heads = width // HD
-    keys = key.shape[1]
-    q_heads = query.reshape(images, rows, heads, HD)
-    k_heads = key.reshape(images, keys, heads, HD)
-    v_heads = value.reshape(images, keys, heads, HD)
-    g_heads = grad_mixed.reshape(images, rows, heads, HD)
-    o_heads = mixed.reshape(images, rows, heads, HD)
-    scores = head_scores(q_heads, k_heads, valid)
-    prob = jnp.exp(scores - log_total)
-    prob_half = prob.astype(bf16)
-    grad_prob = jnp.einsum("bqhd,bkhd->bhqk", g_heads, v_heads, preferred_element_type=f32)
-    delta = jnp.einsum("bqhd,bqhd->bhq", g_heads.astype(f32), o_heads.astype(f32))[..., None]
-    grad_score = (prob * (grad_prob - delta)).astype(bf16)
-    scale = 1.0 / math.sqrt(HD)
-    grad_q = jnp.einsum("bhqk,bkhd->bqhd", grad_score, k_heads, preferred_element_type=f32)
-    grad_k = jnp.einsum("bhqk,bqhd->bkhd", grad_score, q_heads, preferred_element_type=f32)
-    grad_v = jnp.einsum("bhqk,bqhd->bkhd", prob_half, g_heads, preferred_element_type=f32)
-    return (
-        grad_q.reshape(images, rows, width) * scale,
-        grad_k.reshape(images, keys, width) * scale,
-        grad_v.reshape(images, keys, width),
-        grad_score,
-    )
+
+    def whole(shape):
+        return pl.BlockSpec((1,) + shape, lambda i: (i, 0, 0))
+
+    return pl.pallas_call(
+        back_kernel,
+        grid=(images,),
+        in_specs=[whole((seq, wide)), whole((seq, 1)), whole((rows, width)), whole((heads, rows)), whole((rows, width))],
+        out_specs=[whole((seq, wide)), whole((8, wide))],
+        out_shape=[jax.ShapeDtypeStruct((images, seq, wide), bf16), jax.ShapeDtypeStruct((images, 8, wide), f32)],
+        compiler_params=pltpu.CompilerParams(vmem_limit_bytes=56 << 20),
+        cost_estimate=pl.CostEstimate(flops=10*images*rows*seq*width, bytes_accessed=packed.size*4, transcendentals=images*heads*rows*seq),
+    )(packed, valid, mixed, log_total, grad)
 
 
 def body(
@@ -246,16 +283,20 @@
     mask_own = token_mask.astype(f32)
     mask_img = jnp.concatenate([mask_own, y_swap(mask_own)], axis=1)
     mask_all = jnp.concatenate([mask_img, core_swap(mask_img)], axis=0)
-    valid = mask_all > 0
+    valid = mask_all[:, :, None]
 
     attn_half = attn_params.astype(bf16)
     feed_half = feed_params.astype(bf16)
+
+    fill = -3 * half_w % 128
+    packed_w = 3 * half_w + fill
 
     def pick(at):
         parts = [
             attn_half[:, i * width + at * half_w : i * width + (at + 1) * half_w]
             for i in range(4)
         ]
+        parts.insert(3, jnp.zeros((owned, fill), bf16))
         parts.append(attn_half[:, 4 * width :])
         parts.append(feed_half[:, 2 * hidden :])
         for i in range(2):
@@ -270,12 +311,14 @@
         [jnp.where(first_core, keep, got), jnp.where(first_core, got, keep)], axis=0
     )
     vecs = attn_params.shape[1] - 4 * width + feed_params.shape[1] - 2 * hidden
-    cut = 4 * half_w + vecs
+    cut = packed_w + half_w + vecs
     line_a = gather_line(shard[:, :cut], depth)
     sides_a = gather_sides(line_a)
     all_a = gather_corner(sides_a)
     w_attn = gather_all(all_a)
-    line_c = gather_line(after(shard[:, cut : cut + half_h], *sides_a[1:]), depth)
+    line_c = gather_line(after(shard[:, cut : cut + half_h], *line_a), depth)
+    sides_c = gather_sides(line_c, *sides_a[1:])
+    line_d = gather_line(after(shard[:, cut + half_h :], *line_c), depth)
     rows_far = y_swap(after(rows_own, shard))
 
     block = 2 * owned
@@ -286,20 +329,21 @@
     z_of = z_at ^ (place % depth)
     core_of = (spot % block) // owned
     natural = (((z_of * 2 + x_of) * 2 + core_of) * 2 + y_of) * owned + spot % owned
-    row_ids = lax.broadcasted_iota(jnp.int32, (2 * width, width), 0) % width
-    order_two = (row_ids == natural[None, :]).astype(bf16)
-    order = order_two[:width]
+    row_ids = lax.broadcasted_iota(jnp.int32, (width, width), 0)
+    order = (row_ids == natural[None, :]).astype(bf16)
 
     def to_local(values):
-        return mm(split_two(values), order_two)
-
-    order_back = jnp.tile(order.T, (2, 1))
+        both = mm(split_two(values), order)
+        return both[: values.shape[0]] + both[values.shape[0] :]
 
     def to_natural(values):
-        return mm(split_two(values), order_back)
-
-    w_q, w_k, w_v, w_o = (w_attn[:, i * half_w : (i + 1) * half_w] for i in range(4))
-    vec = w_attn[:, 4 * half_w :]
+        both = mm_nt(split_two(values), order)
+        return both[: values.shape[0]] + both[values.shape[0] :]
+
+
+    w_qkv = w_attn[:, :packed_w]
+    w_o = w_attn[:, packed_w : packed_w + half_w]
+    vec = w_attn[:, packed_w + half_w :]
     vec_nat = mm(order, vec[:, 2:4])
     vec_t = vec.astype(f32).T
     gain_one, shift_one, bias_o = vec_t[0], vec_t[1], vec_t[4]
@@ -319,35 +363,41 @@
     half_img = (norm_img * gain_one + shift_one).astype(bf16)
     half_far = core_swap(half_img)
     one_all = jnp.concatenate([half_img, half_far], axis=0)
-    one_own = jnp.concatenate([half_img[:local_len], half_far[:local_len]], axis=0)
     seq = 2 * local_len
-    query = (mm(one_own, w_q) + bias_qv[0]).astype(bf16).reshape(2, local_len, half_w)
-    key = mm(one_all, w_k).astype(bf16).reshape(2, seq, half_w)
-    value = (mm(one_all, w_v) + bias_qv[1]).astype(bf16).reshape(2, seq, half_w)
-    sides_c = gather_sides(line_c, query, key, value)
-    line_d = gather_line(after(shard[:, cut + half_h :], *line_c), depth)
-    query, key, value = after((query, key, value), sides_c[0])
-    mixed, log_total = attend(query, key, value, valid)
-    sides_d = gather_sides(line_d, mixed)
+    gap = jnp.zeros((half_w,), f32)
+    bias_qkv = jnp.concatenate([bias_qv[0], gap, bias_qv[1], gap[:fill]])
+
+    def project(left, right):
+        return (mm(left, right) + bias_qkv).astype(bf16)
+
+    packed = project(one_all, w_qkv).reshape(2, seq, packed_w)
+    mixed, log_total = attend(packed, valid, local_len, half_w)
     all_c = gather_corner(sides_c, mixed)
     w_up = gather_all(all_c)
-    mixed = after(mixed, sides_d[0], *all_c[1:3])
+    sides_d = gather_sides(line_d, mixed, *sides_c[1:])
     mixed_rows = mixed.reshape(2 * local_len, half_w)
     part = mm_nt(mixed_rows, w_o)
     resid = rows_in + part[:local_len] + core_swap(part[local_len:]) + bias_o
 
     norm_two, scale_two = norm_stats(resid)
     half_two = (norm_two * gain_two + shift_two).astype(bf16)
-    all_d = gather_corner(sides_d, half_two)
+    all_d = gather_corner(sides_d)
     w_down = gather_all(all_d)
     two_both = jnp.concatenate([half_two, core_swap(half_two)], axis=0)
-    pre_act = mm(two_both, w_up) + bias_up
-    act_half = gelu_tanh(pre_act).astype(bf16)
+
+    def activate(left, right):
+        values = mm(left, right) + bias_up
+        return values, gelu_tanh(values).astype(bf16)
+
+    pre_act, act_half = activate(two_both, w_up)
     down_corner = scatter_corner(weight_corner(grad_both, act_half), 2)
     down_chunks = weight_chunks(grad_both, act_half)
-    grad_act = mm(after(grad_both, *down_chunks), w_down)
-    grad_pre = jax.vjp(gelu_tanh, pre_act)[1](grad_act)[0]
-    grad_pre_half = grad_pre.astype(bf16)
+
+    def activate_back(left, right):
+        values = jax.vjp(gelu_tanh, pre_act)[1](mm(left, right))[0]
+        return values, values.astype(bf16)
+
+    grad_pre, grad_pre_half = activate_back(after(grad_both, *down_chunks), w_down)
     up_corner = scatter_corner(weight_corner(two_both, grad_pre_half), 0)
     part = mm_nt(grad_pre_half, w_up)
     part_far = core_swap(part[local_len:])
@@ -361,43 +411,21 @@
     resid_both = jnp.concatenate([grad_resid_half, resid_far], axis=0)
 
     grad_mixed = mm(resid_both, w_o).astype(bf16).reshape(2, local_len, half_w)
-    grad_q, grad_k, grad_v, grad_score = attend_back(
-        query, key, value, valid, mixed, log_total, grad_mixed
-    )
-    down_line = scatter_line(down_sides, depth, grad_score)
-    grad_q = grad_q.reshape(2 * local_len, half_w)
-    grad_k = grad_k.reshape(2 * seq, half_w)
-    grad_v = grad_v.reshape(2 * seq, half_w)
-    grad_q_half = grad_q.astype(bf16)
-    grad_k_half = grad_k.astype(bf16)
-    grad_v_half = grad_v.astype(bf16)
+    grad_packed, head_sums = attend_back(packed, valid, mixed, log_total, grad_mixed)
+    grad_packed = grad_packed.reshape(2 * seq, packed_w)
+    down_line = scatter_line(down_sides, depth, grad_packed)
     corner_all = jnp.concatenate(
-        [
-            weight_corner(one_own, grad_q_half),
-            weight_corner(one_all, grad_k_half),
-            weight_corner(one_all, grad_v_half),
-            weight_corner(resid_both, mixed_rows),
-        ],
+        [weight_corner(one_all, grad_packed), weight_corner(resid_both, mixed_rows)],
         axis=1,
     )
     attn_corner = scatter_corner(corner_all, 1)
     up_line = scatter_line(up_sides, depth, corner_all)
-    pieces = [
-        weight_chunks(one_own, grad_q_half),
-        weight_chunks(one_all, grad_k_half),
-        weight_chunks(one_all, grad_v_half),
-        weight_chunks(resid_both, mixed_rows),
-    ]
+    pieces = [weight_chunks(one_all, grad_packed), weight_chunks(resid_both, mixed_rows)]
     attn_chunks = [jnp.concatenate([piece[i] for piece in pieces], axis=1) for i in range(3)]
     attn_sides = scatter_sides(attn_chunks, attn_corner)
-    grad_q_half, grad_k_half, grad_v_half = after(
-        (grad_q_half, grad_k_half, grad_v_half), attn_chunks
-    )
-    part_q = mm_nt(grad_q_half, w_q).reshape(2, local_len, width)
-    part_kv = (mm_nt(grad_k_half, w_k) + mm_nt(grad_v_half, w_v)).reshape(2, seq, width)
-    part_own = jnp.concatenate([part_q[0] + part_kv[0, :local_len], part_kv[0, local_len:]], axis=0)
-    part_sib = jnp.concatenate([part_q[1] + part_kv[1, :local_len], part_kv[1, local_len:]], axis=0)
-    part_img = part_own + core_swap(part_sib)
+    grad_packed = after(grad_packed, attn_chunks)
+    part = mm_nt(grad_packed, w_qkv)
+    part_img = part[:seq] + core_swap(part[seq:])
     part_far = part_img[local_len:].astype(bf16)
     part_far = y_swap(jnp.concatenate([part_far[:, half_w:], part_far[:, :half_w]], axis=1))
     grad_norm_one = part_img[:local_len] + part_far.astype(f32)
@@ -407,8 +435,9 @@
     grad_input = to_natural(grad_in)[None]
 
     zeros = jnp.zeros((half_w,), f32)
-    sum_q = jnp.sum(grad_q, axis=0)
-    sum_v = jnp.sum(grad_v, axis=0)
+    head_sum = jnp.sum(head_sums[:, 0], axis=0)
+    sum_q = head_sum[:half_w]
+    sum_v = head_sum[2 * half_w : 3 * half_w]
 
     def spread(vector):
         return jnp.where(
@@ -471,11 +500,8 @@
     vec_sum = lax.dynamic_slice_in_dim(cols.T, device_at * owned, owned, axis=0)
     grad_attn = jnp.concatenate(
         [
-            join(
-                attn_mine[:, i * half_w : (i + 1) * half_w],
-                attn_other[:, i * half_w : (i + 1) * half_w],
-            )
-            for i in range(4)
+            join(attn_mine[:, at : at + half_w], attn_other[:, at : at + half_w])
+            for at in (0, half_w, 2 * half_w, packed_w)
         ]
         + [vec_sum[:, :2], vec_sum[:, 6:8], vec_sum[:, 2:3]],
         axis=1,

time: 643 us -> 559 us (0.87)
  the two profiles are of different devices: /device:TPU:1 before, /device:TPU:0 now
where the time goes in v1:
time: 559 us; the launch traced here: 548 us
  waiting for transfers between devices  212 us (38%)
  matrix products  116 us (21%)
  starting transfers between devices  78.6 us (14%)
  other arithmetic  54.3 us (10%)
  local copies, waits for them, and re-layouts  48.4 us (9%)
  Pallas kernels  35.8 us (6%)
    ppermute x46, waiting for transfers between devices, dp_swap(): return lax.ppermute(value, 'dp', [(i, i ^ mask) for i in range(count)])  113 us
    ppermute x15, waiting for transfers between devices, y_swap(): return lax.ppermute(value, 'ctx', [(i, i ^ 1) for i in range(count)])  99.6 us
    ppermute x46, starting transfers between devices, dp_swap(): return lax.ppermute(value, 'dp', [(i, i ^ mask) for i in range(count)])  63 us
    dot_general x7, matrix products, mm(): return jnp.dot(left, right, preferred_element_type=f32)  44.5 us
    dot_general x16, matrix products, mm_tn(): lax.dot_general(left, right, (((0,), (0,)), ((), ())), preferred_element_...  37.2 us
    dot_general x7, matrix products, mm_nt(): lax.dot_general(left, right, (((1,), (1,)), ((), ())), preferred_element_...  34.2 us
    pallas_call x1, Pallas kernels, attend_back(): pl.pallas_call(back_kernel, grid=(images,), in_specs=[whole((seq, wide)),...  21 us
    unnamed x137, local copies, waits for them, and re-layouts  16.3 us
  transfers between devices with their start and end apart: 61, of which 23 were waited for; matrix products, arithmetic and copies ran while one was open for 31% of the time, Pallas kernels for 4%

profile of v1, /device:TPU:0, one launch (start us, length us, event | category | flops | bytes accessed | tf_op | source)
XLA Modules:
  0.0 548.0 jit_solution(1825417149760849641)
XLA Ops:
  17.3 7.9 %collective-permute-done.4 = bf16[72,2376]{1,0:T(8,128)(2,1)S(1)} collective-permute-done((bf16[72,2376]{1,0:T(8,128)(2,1)S(1)}, bf16[72,2376]{1,0:T(8,128)(2,1)S(1)}, u32[]{:S(2)}, u32[]{:S(2)}) %collective-permute-start.4) | collective-permute-done | bytes 342176 | tf_op jit(solution)/shard_map/ppermute | solution.py:72
  25.2 20.8 %collective-permute-done.3 = bf16[72,2376]{1,0:T(8,128)(2,1)S(1)} collective-permute-done((bf16[72,2376]{1,0:T(8,128)(2,1)S(1)}, bf16[72,2376]{1,0:T(8,128)(2,1)S(1)}, u32[]{:S(2)}, u32[]{:S(2)}) %collective-permute-start.3) | collective-permute-done | bytes 342176 | tf_op jit(solution)/shard_map/ppermute | solution.py:72
  59.6 14.2 %collective-permute-done.15 = bf16[72,2152]{1,0:T(8,128)(2,1)S(1)} collective-permute-done((bf16[72,2152]{1,0:T(8,128)(2,1)S(1)}, bf16[72,2152]{1,0:T(8,128)(2,1)S(1)}, u32[]{:S(2)}, u32[]{:S(2)}) %collective-permute-start.15) | collective-permute-done | bytes 309920 | tf_op jit(solution)/shard_map/ppermute | solution.py:72
  81.6 6.2 %collective-permute-done.5 = bf16[288,2376]{1,0:T(8,128)(2,1)S(1)} collective-permute-done((bf16[288,2376]{1,0:T(8,128)(2,1)S(1)}, bf16[288,2376]{1,0:T(8,128)(2,1)S(1)}, u32[]{:S(2)}, u32[]{:S(2)}) %collective-permute-start.5) | collective-permute-done | bytes 1368608 | tf_op jit(solution)/shard_map/ppermute | solution.py:72
  90.9 10.2 %collective-permute-done.7 = bf16[144,2376]{1,0:T(8,128)(2,1)S(1)} collective-permute-done((bf16[144,2376]{1,0:T(8,128)(2,1)S(1)}, bf16[144,2376]{1,0:T(8,128)(2,1)S(1)}, u32[]{:S(2)}, u32[]{:S(2)}) %collective-permute-start.7) | collective-permute-done | bytes 684320 | tf_op jit(solution)/shard_map/ppermute | solution.py:89
  101.1 10.7 %collective-permute-start.22 = (bf16[72,2152]{1,0:T(8,128)(2,1)S(1)}, bf16[72,2152]{1,0:T(8,128)(2,1)S(1)}, u32[]{:S(2)}, u32[]{:S(2)}) collective-permute-start(bf16[72,2152]{1,0:T(8,128)(2,1)S(1)} %get-tuple-element.75), channel_id=1, source_target_pairs={{0,8},{2,10},{4,12},{6,14},{8,0},{10,2},{12,4},{14,6},{16,24},{18,... | collective-permute-start | bytes 929672 | tf_op jit(solution)/shard_map/ppermute | solution.py:72
  123.3 23.9 %collective-permute-done.18 = bf16[288,2152]{1,0:T(8,128)(2,1)} collective-permute-done((bf16[288,2152]{1,0:T(8,128)(2,1)S(1)}, bf16[288,2152]{1,0:T(8,128)(2,1)}, u32[]{:S(2)}, u32[]{:S(2)}) %collective-permute-start.18) | collective-permute-done | bytes 1239584 | tf_op jit(solution)/shard_map/ppermute | solution.py:89
  152.0 12.4 %add_convert_fusion = bf16[1536,1792]{1,0:T(8,128)(2,1)} fusion(f32[1792]{0:T(1024)S(1)} %concatenate.165, bf16[1152,2376]{1,0:T(8,128)(2,1)} %copy-done.24, bf16[768,1152]{1,0:T(8,128)(2,1)} %collective-permute-done.9, bf16[768,1152]{1,0:T(8,128)(2,1)} %get-tuple-element.148), kind=kOutput, calls=%fused_computation | convolution fusion | flops 6354370560 | bytes 13179904 | tf_op jit(solution)/shard_map/dot_general | solution.py:59
  164.3 14.8 %shard_map.227 = (bf16[2,384,576]{2,1,0:T(8,128)(2,1)}, f32[2,8,384]{2,1,0:T(8,128)}) custom-call(bf16[2,768,1792]{2,1,0:T(8,128)(2,1)} %bitcast.59, f32[2,768,1]{2,1,0:T(8,128)} %copy.29.valid_ref), custom_call_target="tpu_custom_call" | custom-call | flops 1358954496 | bytes 5505024 | tf_op jit(solution)/shard_map/pallas_call | solution.py:191
  189.3 32.3 %collective-permute-done.19 = bf16[144,2152]{1,0:T(8,128)(2,1)S(1)} collective-permute-done((bf16[144,2152]{1,0:T(8,128)(2,1)S(1)}, bf16[144,2152]{1,0:T(8,128)(2,1)S(1)}, u32[]{:S(2)}, u32[]{:S(2)}) %collective-permute-start.19) | collective-permute-done | bytes 619808 | tf_op jit(solution)/shard_map/ppermute | solution.py:89
  227.6 10.8 %collective-permute-done.27 = bf16[144,2152]{1,0:T(8,128)(2,1)S(1)} collective-permute-done((bf16[144,2152]{1,0:T(8,128)(2,1)S(1)}, bf16[144,2152]{1,0:T(8,128)(2,1)S(1)}, u32[]{:S(2)}, u32[]{:S(2)}) %collective-permute-start.27) | collective-permute-done | bytes 619808 | tf_op jit(solution)/shard_map/ppermute | solution.py:89
  238.8 8.8 %multiply_convert_fusion = (bf16[768,2152]{0,1:T(8,128)(2,1)S(1)}, f32[768,2152]{0,1:T(8,128)}) fusion(f32[2152]{0:T(1024)S(1)} %slice_select_fusion.6, bf16[1152,2152]{1,0:T(8,128)(2,1)S(1)} %bitcast.57, bf16[384,1152]{1,0:T(8,128)(2,1)S(1)} %collective-permute-done.13, bf16[384,1152]{1,0:T(8,128)(2,1)S(1)} %add_convert_fusion.7), kind=kOutput, calls=%fused_computation.9 | convolution fusion | flops 3827970048 | bytes 16652704 | tf_op jit(solution)/shard_map/dot_general | solution.py:59
  256.9 13.1 %fusion.148 = (f32[2152]{0:T(1024)}, bf16[768,2152]{0,1:T(8,128)(2,1)}) fusion(f32[768,2152]{0,1:T(8,128)} %get-tuple-element.207, f32[2152]{0:T(1024)S(1)} %slice_select_fusion.6, bf16[768,1152]{1,0:T(8,128)(2,1)S(1)} %copy-done.13, bf16[1152,2152]{1,0:T(8,128)(2,1)S(1)} %constant_dynamic-update-slice_fusion.10), kind=kOutput, calls=%fused_computation.350 | convolution fusion | flops 3844261888 | bytes 16661312 | tf_op jit(solution)/shard_map/dot_general | solution.py:59
  270.0 6.8 %fusion.165 = f32[768,1152]{1,0:T(8,128)S(1)} fusion(bf16[768,2152]{0,1:T(8,128)(2,1)} %get-tuple-element.79, bf16[1152,2152]{1,0:T(8,128)(2,1)S(1)} %bitcast.57), kind=kOutput, calls=%fused_computation.364 | convolution fusion | flops 3807903744 | bytes 11802624 | tf_op jit(solution)/shard_map/dot_general | solution.py:63
  291.1 17.8 %collective-permute-done.54 = bf16[288,2152]{1,0:T(8,128)(2,1)S(1)} collective-permute-done((bf16[288,2152]{1,0:T(8,128)(2,1)S(1)}, bf16[288,2152]{1,0:T(8,128)(2,1)S(1)}, u32[]{:S(2)}, u32[]{:S(2)}) %collective-permute-start.54) | collective-permute-done | bytes 1239584 | tf_op jit(solution)/shard_map/ppermute | solution.py:89
  326.2 21.0 %shard_map.228 = (bf16[2,768,1792]{2,1,0:T(8,128)(2,1)}, f32[2,8,1792]{2,1,0:T(8,128)}) custom-call(bf16[2,768,1792]{2,1,0:T(8,128)(2,1)} %bitcast.60, f32[2,768,1]{2,1,0:T(8,128)} %copy.29.valid_ref, bf16[2,384,576]{2,1,0:T(8,128)(2,1)} %get-tuple-element.67.mixed_ref, f32[2,8,384]{2,1,0:T(8,128)} %get-tuple-element.72.log_ref, bf16[2,384,576]{2,1,0:T(8,128)(2,1)} %bitcast.48), custom_call_target="tpu_custom_call" | custom-call | flops 3397386240 | bytes 11010048 | tf_op jit(solution)/shard_map/pallas_call | solution.py:241
  347.9 5.0 convolution_convert_fusion.11
  373.2 9.5 %fusion.12 = f32[1536,1152]{1,0:T(8,128)S(1)} fusion(bf16[1536,1792]{1,0:T(8,128)(2,1)} %bitcast.62, bf16[1152,2376]{1,0:T(8,128)(2,1)S(1)} %bitcast.52), kind=kOutput, calls=%fused_computation.34 | convolution fusion | flops 6341787648 | bytes 16711680 | tf_op jit(solution)/shard_map/dot_general | solution.py:63
  382.7 7.3 %fusion.166 = f32[768,1152]{1,0:T(8,128)S(1)} fusion(bf16[768,2152]{0,1:T(8,128)(2,1)S(1)} %copy-done.52, bf16[1152,2152]{1,0:T(8,128)(2,1)} %copy-done.37), kind=kOutput, calls=%fused_computation.365 | convolution fusion | flops 3807903744 | bytes 11802624 | tf_op jit(solution)/shard_map/dot_general | solution.py:63
  409.8 13.0 %collective-permute-start.50 = (bf16[72,2152]{1,0:T(8,128)(2,1)S(1)}, bf16[72,2152]{1,0:T(8,128)(2,1)S(1)}, u32[]{:S(2)}, u32[]{:S(2)}) collective-permute-start(bf16[72,2152]{1,0:T(8,128)(2,1)S(1)} %get-tuple-element.169), channel_id=1, source_target_pairs={{0,8},{2,10},{4,12},{6,14},{8,0},{10,2},{12,4},{14,6},{16,24},{18,... | collective-permute-start | bytes 929672 | tf_op jit(solution)/shard_map/ppermute | solution.py:72
  429.2 11.9 %collective-permute-done.50 = bf16[72,2152]{1,0:T(8,128)(2,1)S(1)} collective-permute-done((bf16[72,2152]{1,0:T(8,128)(2,1)S(1)}, bf16[72,2152]{1,0:T(8,128)(2,1)S(1)}, u32[]{:S(2)}, u32[]{:S(2)}) %collective-permute-start.50) | collective-permute-done | bytes 309920 | tf_op jit(solution)/shard_map/ppermute | solution.py:72
  446.3 10.5 %collective-permute-done.58 = bf16[72,2152]{1,0:T(8,128)(2,1)S(1)} collective-permute-done((bf16[72,2152]{1,0:T(8,128)(2,1)S(1)}, bf16[72,2152]{1,0:T(8,128)(2,1)S(1)}, u32[]{:S(2)}, u32[]{:S(2)}) %collective-permute-start.58) | collective-permute-done | bytes 309920 | tf_op jit(solution)/shard_map/ppermute | solution.py:72
  475.4 13.9 %collective-permute-done.44 = f32[1,11368]{1,0:T(1,128)S(1)} collective-permute-done((f32[1,11368]{1,0:T(1,128)S(1)}, f32[1,11368]{1,0:T(1,128)S(1)}, u32[]{:S(2)}, u32[]{:S(2)}) %collective-permute-start.44) | collective-permute-done | bytes 45504 | tf_op jit(solution)/shard_map/ppermute | solution.py:72
  493.3 11.3 %collective-permute-done.45 = f32[1,11368]{1,0:T(1,128)S(1)} collective-permute-done((f32[1,11368]{1,0:T(1,128)S(1)}, f32[1,11368]{1,0:T(1,128)S(1)}, u32[]{:S(2)}, u32[]{:S(2)}) %collective-permute-start.45) | collective-permute-done | bytes 45504 | tf_op jit(solution)/shard_map/ppermute | solution.py:72
  (408 shorter events, 231.4 us)
Async XLA Ops:
  16.6 58.8 %collective-permute-start.1 = (bf16[384,1152]{1,0:T(8,128)(2,1)S(1)}, bf16[384,1152]{1,0:T(8,128)(2,1)S(1)}, u32[]{:S(2)}, u32[]{:S(2)}) collective-permute-start(bf16[384,1152]{1,0:T(8,128)(2,1)S(1)} %bitcast.49), channel_id=1, source_target_pairs={{0,1},{1,0},{2,3},{3,2},{4,5},{5,4},{6,7},{7,6},{8,9},{9,8},{10,11... | collective-permute-start | bytes 2654216 | tf_op jit(solution)/shard_map/ppermute | solution.py:89
  73.8 45.4 %collective-permute-start.21 = (bf16[384,1152]{1,0:T(8,128)(2,1)S(1)}, bf16[384,1152]{1,0:T(8,128)(2,1)S(1)}, u32[]{:S(2)}, u32[]{:S(2)}) collective-permute-start(bf16[384,1152]{1,0:T(8,128)(2,1)S(1)} %fusion.143), channel_id=1, source_target_pairs={{0,2},{2,0},{4,6},{6,4},{8,10},{10,8},{12,14},{14,12},{16,18},{18,... | collective-permute-start | bytes 2654216 | tf_op jit(solution)/shard_map/ppermute | solution.py:72
  73.8 43.2 %collective-permute-start.24 = (bf16[72,2152]{1,0:T(8,128)(2,1)S(1)}, bf16[72,2152]{1,0:T(8,128)(2,1)S(1)}, u32[]{:S(2)}, u32[]{:S(2)}) collective-permute-start(bf16[72,2152]{1,0:T(8,128)(2,1)S(1)} %get-tuple-element.75), channel_id=1, source_target_pairs={{0,24},{2,26},{4,28},{6,30},{8,16},{10,18},{12,20},{14,22},{16,8},... | collective-permute-start | bytes 929672 | tf_op jit(solution)/shard_map/ppermute | solution.py:72
  75.4 41.6 %collective-permute-start.23 = (bf16[72,2152]{1,0:T(8,128)(2,1)S(1)}, bf16[72,2152]{1,0:T(8,128)(2,1)S(1)}, u32[]{:S(2)}, u32[]{:S(2)}) collective-permute-start(bf16[72,2152]{1,0:T(8,128)(2,1)S(1)} %get-tuple-element.75), channel_id=1, source_target_pairs={{0,16},{2,18},{4,20},{6,22},{8,24},{10,26},{12,28},{14,30},{16,0},... | collective-permute-start | bytes 929672 | tf_op jit(solution)/shard_map/ppermute | solution.py:72
  117.0 35.0 %collective-permute-start.9 = (bf16[768,1152]{1,0:T(8,128)(2,1)}, bf16[768,1152]{1,0:T(8,128)(2,1)}, u32[]{:S(2)}, u32[]{:S(2)}) collective-permute-start(bf16[768,1152]{1,0:T(8,128)(2,1)} %get-tuple-element.148), channel_id=1, source_target_pairs={{0,2},{2,0},{4,6},{6,4},{8,10},{10,8},{12,14},{14,12},{16,18},{18,... | collective-permute-start | bytes 5308424 | tf_op jit(solution)/shard_map/ppermute | solution.py:72
  179.1 44.3 %collective-permute-start.26 = (bf16[288,2152]{1,0:T(8,128)(2,1)S(1)}, bf16[288,2152]{1,0:T(8,128)(2,1)S(1)}, u32[]{:S(2)}, u32[]{:S(2)}) collective-permute-start(bf16[288,2152]{1,0:T(8,128)(2,1)S(1)} %pad_maximum_fusion.19), channel_id=1, source_target_pairs={{0,1},{1,0},{2,3},{3,2},{4,5},{5,4},{6,7},{7,6},{8,9},{9,8},{10,11... | collective-permute-start | bytes 3718664 | tf_op jit(solution)/shard_map/ppermute | solution.py:89
  179.8 43.7 %collective-permute-start.25 = (bf16[288,2152]{1,0:T(8,128)(2,1)S(1)}, bf16[288,2152]{1,0:T(8,128)(2,1)S(1)}, u32[]{:S(2)}, u32[]{:S(2)}) collective-permute-start(bf16[288,2152]{1,0:T(8,128)(2,1)S(1)} %pad_maximum_fusion.19), channel_id=1, source_target_pairs={{0,4},{2,6},{4,0},{6,2},{8,12},{10,14},{12,8},{14,10},{16,20},{18,... | collective-permute-start | bytes 3718664 | tf_op jit(solution)/shard_map/ppermute | solution.py:72
  181.3 40.4 %collective-permute-start.19 = (bf16[144,2152]{1,0:T(8,128)(2,1)S(1)}, bf16[144,2152]{1,0:T(8,128)(2,1)S(1)}, u32[]{:S(2)}, u32[]{:S(2)}) collective-permute-start(bf16[144,2152]{1,0:T(8,128)(2,1)S(1)} %slice.529), channel_id=1, source_target_pairs={{0,1},{1,0},{2,3},{3,2},{4,5},{5,4},{6,7},{7,6},{8,9},{9,8},{10,11... | collective-permute-start | bytes 1859336 | tf_op jit(solution)/shard_map/ppermute | solution.py:89
  186.2 40.0 %collective-permute-start.12 = (f32[384,1152]{1,0:T(8,128)S(1)}, f32[384,1152]{1,0:T(8,128)S(1)}, u32[]{:S(2)}, u32[]{:S(2)}) collective-permute-start(f32[384,1152]{1,0:T(8,128)S(1)} %slice.523), channel_id=1, source_target_pairs={{0,2},{2,0},{4,6},{6,4},{8,10},{10,8},{12,14},{14,12},{16,18},{18,... | collective-permute-start | bytes 5308424 | tf_op jit(solution)/shard_map/ppermute | solution.py:72
  188.7 33.9 %collective-permute-start.20 = (bf16[144,2152]{1,0:T(8,128)(2,1)S(1)}, bf16[144,2152]{1,0:T(8,128)(2,1)S(1)}, u32[]{:S(2)}, u32[]{:S(2)}) collective-permute-start(bf16[144,2152]{1,0:T(8,128)(2,1)S(1)} %slice.530), channel_id=1, source_target_pairs={{0,4},{2,6},{4,0},{6,2},{8,12},{10,14},{12,8},{14,10},{16,20},{18,... | collective-permute-start | bytes 1859336 | tf_op jit(solution)/shard_map/ppermute | solution.py:72
  250.9 110.7 %collective-permute-start.56 = (bf16[288,2152]{1,0:T(8,128)(2,1)}, bf16[288,2152]{1,0:T(8,128)(2,1)}, u32[]{:S(2)}, u32[]{:S(2)}) collective-permute-start(bf16[288,2152]{1,0:T(8,128)(2,1)} %convolution_convert_fusion.5), channel_id=1, source_target_pairs={{0,1},{1,0},{2,3},{3,2},{4,5},{5,4},{6,7},{7,6},{8,9},{9,8},{10,11... | collective-permute-start | bytes 3718664 | tf_op jit(solution)/shard_map/ppermute | solution.py:89
  277.0 31.9 %collective-permute-start.29 = (f32[384,1152]{1,0:T(8,128)S(1)}, f32[384,1152]{1,0:T(8,128)S(1)}, u32[]{:S(2)}, u32[]{:S(2)}) collective-permute-start(f32[384,1152]{1,0:T(8,128)S(1)} %slice.548), channel_id=1, source_target_pairs={{0,2},{2,0},{4,6},{6,4},{8,10},{10,8},{12,14},{14,12},{16,18},{18,... | collective-permute-start | bytes 5308424 | tf_op jit(solution)/shard_map/ppermute | solution.py:72
  281.4 36.0 %collective-permute-start.48 = (bf16[288,2152]{1,0:T(8,128)(2,1)S(1)}, bf16[288,2152]{1,0:T(8,128)(2,1)S(1)}, u32[]{:S(2)}, u32[]{:S(2)}) collective-permute-start(bf16[288,2152]{1,0:T(8,128)(2,1)S(1)} %convolution_convert_fusion.1), channel_id=1, source_target_pairs={{0,4},{2,6},{4,0},{6,2},{8,12},{10,14},{12,8},{14,10},{16,20},{18,... | collective-permute-start | bytes 3718664 | tf_op jit(solution)/shard_map/ppermute | solution.py:72
  285.8 108.7 %collective-permute-start.47 = (bf16[288,2152]{1,0:T(8,128)(2,1)}, bf16[288,2152]{1,0:T(8,128)(2,1)S(1)}, u32[]{:S(2)}, u32[]{:S(2)}) collective-permute-start(bf16[288,2152]{1,0:T(8,128)(2,1)} %convolution_convert_fusion.3), channel_id=1, source_target_pairs={{0,4},{2,6},{4,0},{6,2},{8,12},{10,14},{12,8},{14,10},{16,20},{18,... | collective-permute-start | bytes 3718664 | tf_op jit(solution)/shard_map/ppermute | solution.py:72
  313.5 51.4 %collective-permute-start.55 = (bf16[288,2152]{1,0:T(8,128)(2,1)}, bf16[288,2152]{1,0:T(8,128)(2,1)}, u32[]{:S(2)}, u32[]{:S(2)}) collective-permute-start(bf16[288,2152]{1,0:T(8,128)(2,1)} %add_convert_fusion.4), channel_id=1, source_target_pairs={{0,4},{2,6},{4,0},{6,2},{8,12},{10,14},{12,8},{14,10},{16,20},{18,... | collective-permute-start | bytes 3718664 | tf_op jit(solution)/shard_map/ppermute | solution.py:72
  318.8 75.7 %collective-permute-start.49 = (bf16[288,2152]{1,0:T(8,128)(2,1)}, bf16[288,2152]{1,0:T(8,128)(2,1)}, u32[]{:S(2)}, u32[]{:S(2)}) collective-permute-start(bf16[288,2152]{1,0:T(8,128)(2,1)} %add_convert_fusion.6), channel_id=1, source_target_pairs={{0,1},{1,0},{2,3},{3,2},{4,5},{5,4},{6,7},{7,6},{8,9},{9,8},{10,11... | collective-permute-start | bytes 3718664 | tf_op jit(solution)/shard_map/ppermute | solution.py:89
  394.5 46.6 %collective-permute-start.32 = (f32[768,1152]{1,0:T(8,128)S(1)}, f32[768,1152]{1,0:T(8,128)S(1)}, u32[]{:S(2)}, u32[]{:S(2)}) collective-permute-start(f32[768,1152]{1,0:T(8,128)S(1)} %slice.571), channel_id=1, source_target_pairs={{0,2},{2,0},{4,6},{6,4},{8,10},{10,8},{12,14},{14,12},{16,18},{18,... | collective-permute-start | bytes 10616840 | tf_op jit(solution)/shard_map/ppermute | solution.py:72
  400.9 56.1 %collective-permute-start.37 = (bf16[288,2368]{1,0:T(8,128)(2,1)S(1)}, bf16[288,2368]{1,0:T(8,128)(2,1)S(1)}, u32[]{:S(2)}, u32[]{:S(2)}) collective-permute-start(bf16[288,2368]{1,0:T(8,128)(2,1)S(1)} %pad_maximum_fusion.16), channel_id=1, source_target_pairs={{0,1},{1,0},{2,3},{3,2},{4,5},{5,4},{6,7},{7,6},{8,9},{9,8},{10,11... | collective-permute-start | bytes 4091912 | tf_op jit(solution)/shard_map/ppermute | solution.py:89
  402.1 55.4 %collective-permute-start.36 = (bf16[288,2368]{1,0:T(8,128)(2,1)S(1)}, bf16[288,2368]{1,0:T(8,128)(2,1)S(1)}, u32[]{:S(2)}, u32[]{:S(2)}) collective-permute-start(bf16[288,2368]{1,0:T(8,128)(2,1)S(1)} %pad_maximum_fusion.15), channel_id=1, source_target_pairs={{0,4},{2,6},{4,0},{6,2},{8,12},{10,14},{12,8},{14,10},{16,20},{18,... | collective-permute-start | bytes 4091912 | tf_op jit(solution)/shard_map/ppermute | solution.py:72
  409.8 31.3 %collective-permute-start.50 = (bf16[72,2152]{1,0:T(8,128)(2,1)S(1)}, bf16[72,2152]{1,0:T(8,128)(2,1)S(1)}, u32[]{:S(2)}, u32[]{:S(2)}) collective-permute-start(bf16[72,2152]{1,0:T(8,128)(2,1)S(1)} %get-tuple-element.169), channel_id=1, source_target_pairs={{0,8},{2,10},{4,12},{6,14},{8,0},{10,2},{12,4},{14,6},{16,24},{18,... | collective-permute-start | bytes 929672 | tf_op jit(solution)/shard_map/ppermute | solution.py:72
  470.1 46.6 %collective-permute-start.53 = (f32[36,2152]{1,0:T(8,128)}, f32[36,2152]{1,0:T(8,128)}, u32[]{:S(2)}, u32[]{:S(2)}) collective-permute-start(f32[36,2152]{1,0:T(8,128)} %get-tuple-element.182), channel_id=1, source_target_pairs={{0,2},{2,0},{4,6},{6,4},{8,10},{10,8},{12,14},{14,12},{16,18},{18,... | collective-permute-start | bytes 929672 | tf_op jit(solution)/shard_map/ppermute | solution.py:72
  470.2 49.9 %collective-permute-start.60 = (f32[36,2152]{1,0:T(8,128)}, f32[36,2152]{1,0:T(8,128)}, u32[]{:S(2)}, u32[]{:S(2)}) collective-permute-start(f32[36,2152]{1,0:T(8,128)} %get-tuple-element.180), channel_id=1, source_target_pairs={{0,2},{2,0},{4,6},{6,4},{8,10},{10,8},{12,14},{14,12},{16,18},{18,... | collective-permute-start | bytes 929672 | tf_op jit(solution)/shard_map/ppermute | solution.py:72
  470.7 54.0 %collective-permute-start.40 = (bf16[72,2368]{1,0:T(8,128)(2,1)}, bf16[72,2368]{1,0:T(8,128)(2,1)}, u32[]{:S(2)}, u32[]{:S(2)}) collective-permute-start(bf16[72,2368]{1,0:T(8,128)(2,1)} %get-tuple-element.157), channel_id=1, source_target_pairs={{0,24},{2,26},{4,28},{6,30},{8,16},{10,18},{12,20},{14,22},{16,8},... | collective-permute-start | bytes 1022984 | tf_op jit(solution)/shard_map/ppermute | solution.py:72
  472.9 51.8 %collective-permute-start.39 = (bf16[72,2368]{1,0:T(8,128)(2,1)}, bf16[72,2368]{1,0:T(8,128)(2,1)}, u32[]{:S(2)}, u32[]{:S(2)}) collective-permute-start(bf16[72,2368]{1,0:T(8,128)(2,1)} %get-tuple-element.158), channel_id=1, source_target_pairs={{0,16},{2,18},{4,20},{6,22},{8,24},{10,26},{12,28},{14,30},{16,0},... | collective-permute-start | bytes 1022984 | tf_op jit(solution)/shard_map/ppermute | solution.py:72
  (98 other events, 1521.6 us)

commit v2 on v1

--- a/solution.py
+++ b/solution.py
@@ -313,13 +313,13 @@
     vecs = attn_params.shape[1] - 4 * width + feed_params.shape[1] - 2 * hidden
     cut = packed_w + half_w + vecs
     line_a = gather_line(shard[:, :cut], depth)
-    sides_a = gather_sides(line_a)
+    rows_far = y_swap(after(rows_own, shard))
+    sides_a = gather_sides(line_a, rows_far)
     all_a = gather_corner(sides_a)
     w_attn = gather_all(all_a)
     line_c = gather_line(after(shard[:, cut : cut + half_h], *line_a), depth)
     sides_c = gather_sides(line_c, *sides_a[1:])
     line_d = gather_line(after(shard[:, cut + half_h :], *line_c), depth)
-    rows_far = y_swap(after(rows_own, shard))
 
     block = 2 * owned
     spot = after(jnp.arange(width, dtype=jnp.int32), shard)
@@ -359,8 +359,12 @@
 
     rows_img = mm(after(jnp.concatenate([rows_own, rows_far], axis=0), sides_a[0]), order)
     rows_in = rows_img[:local_len]
-    norm_img, scale_img = norm_stats(rows_img)
-    half_img = (norm_img * gain_one + shift_one).astype(bf16)
+
+    def norm_one(values):
+        normed, inv_std = norm_stats(values)
+        return normed, inv_std, (normed * gain_one + shift_one).astype(bf16)
+
+    norm_img, scale_img, half_img = norm_one(rows_img)
     half_far = core_swap(half_img)
     one_all = jnp.concatenate([half_img, half_far], axis=0)
     seq = 2 * local_len
@@ -390,8 +394,10 @@
         return values, gelu_tanh(values).astype(bf16)
 
     pre_act, act_half = activate(two_both, w_up)
-    down_corner = scatter_corner(weight_corner(grad_both, act_half), 2)
+    down_last = weight_corner(grad_both, act_half)
     down_chunks = weight_chunks(grad_both, act_half)
+    down_last, down_chunks = after((down_last, down_chunks), *sides_d[1:])
+    down_corner = scatter_corner(down_last, 2)
 
     def activate_back(left, right):
         values = jax.vjp(gelu_tanh, pre_act)[1](mm(left, right))[0]
@@ -409,6 +415,30 @@
     resid_far = core_swap(grad_resid_half)
     up_sides = scatter_sides(up_chunks, up_corner, grad_resid_half)
     resid_both = jnp.concatenate([grad_resid_half, resid_far], axis=0)
+
+    def butterfly(values):
+        values = values + y_swap(values)
+        mask = 2
+        while mask < dp_count:
+            values = values + dp_swap(values, mask)
+            mask = 2 * mask
+        return values, core_swap(values)
+
+    early = jnp.concatenate(
+        [
+            jnp.sum(grad_resid, axis=0, keepdims=True),
+            jnp.sum(grad_norm_two * norm_two, axis=0, keepdims=True),
+            jnp.sum(grad_norm_two, axis=0, keepdims=True),
+            jnp.sum(grad_rows, axis=0, keepdims=True),
+        ],
+        axis=0,
+    )
+    early = jnp.concatenate(
+        [to_natural(early).reshape(1, -1), jnp.sum(grad_pre, axis=0, keepdims=True)], axis=1
+    )
+    early_sum, early_far = butterfly(early)
+    early_cols = (early_sum + early_far)[:, : 4 * width].reshape(4, width)
+    bias_mine, bias_far = early_sum[:, 4 * width :], early_far[:, 4 * width :]
 
     grad_mixed = mm(resid_both, w_o).astype(bf16).reshape(2, local_len, half_w)
     grad_packed, head_sums = attend_back(packed, valid, mixed, log_total, grad_mixed)
@@ -446,37 +476,25 @@
             jnp.concatenate([zeros, vector]),
         )
 
-    cols = jnp.stack(
+    late = jnp.concatenate(
         [
-            jnp.sum(part_img * norm_img, axis=0),
-            jnp.sum(part_img, axis=0),
-            jnp.sum(grad_resid, axis=0),
-            jnp.sum(grad_norm_two * norm_two, axis=0),
-            jnp.sum(grad_norm_two, axis=0),
-            jnp.sum(grad_rows, axis=0),
+            jnp.sum(part_img * norm_img, axis=0, keepdims=True),
+            jnp.sum(part_img, axis=0, keepdims=True),
         ],
         axis=0,
     )
-    cols = to_natural(cols).reshape(1, -1)
-    bias_sum = jnp.sum(grad_pre, axis=0, keepdims=True)
-    sums = jnp.concatenate(
-        [cols, spread(sum_q)[None], spread(sum_v)[None], bias_sum], axis=1
-    )
-    sums = sums + y_swap(sums)
-    mask = 2
-    while mask < dp_count:
-        sums = sums + dp_swap(sums, mask)
-        mask *= 2
-    sums_far = core_swap(sums)
-    cols = (sums + sums_far)[0, : 8 * width].reshape(8, width)
-    bias_mine, bias_far = sums[:, 8 * width :], sums_far[:, 8 * width :]
+    late = jnp.concatenate(
+        [to_natural(late).reshape(1, -1), spread(sum_q)[None], spread(sum_v)[None]], axis=1
+    )
+    late_sum, late_far = butterfly(late)
+    late_cols = (late_sum + late_far).reshape(4, width)
 
     down_sum = scatter_done(down_line, part_img)
     up_sum = scatter_done(up_line, part_img)
-    attn_line = scatter_line(attn_sides, depth, part_img)
+    attn_line = scatter_line(attn_sides, depth, late)
     attn_sum = scatter_done(attn_line)
 
-    part_out = mm_nt(after(act_half, *attn_chunks), w_down)
+    part_out = mm_nt(after(act_half, late), w_down)
     block_rows = resid + part_out[:local_len] + core_swap(part_out[local_len:]) + bias_d
     block_out = to_natural(block_rows)[None]
 
@@ -493,29 +511,31 @@
             jnp.concatenate([other, mine], axis=1),
         )
 
-    down_mine, down_other = trade(down_sum)
-    up_mine, up_other = trade(up_sum)
+    device_at = dp_at * ctx_count + y_at
+
+    def own_rows(values):
+        return lax.dynamic_slice_in_dim(values.T, device_at * owned, owned, axis=0)
+
+    def finish_feed(down_sum, up_sum, early_cols):
+        grad = jnp.concatenate(
+            [join(*trade(up_sum)), join(*trade(down_sum)), own_rows(early_cols)[:, 1:]], axis=1
+        )
+        return (grad,) + adamw_step(feed_params, feed_first, feed_second, grad)
+
+    grad_feed, new_feed, new_feed_first, new_feed_second = finish_feed(down_sum, up_sum, early_cols)
     attn_mine, attn_other = trade(attn_sum)
-    device_at = dp_at * ctx_count + y_at
-    vec_sum = lax.dynamic_slice_in_dim(cols.T, device_at * owned, owned, axis=0)
     grad_attn = jnp.concatenate(
         [
             join(attn_mine[:, at : at + half_w], attn_other[:, at : at + half_w])
             for at in (0, half_w, 2 * half_w, packed_w)
         ]
-        + [vec_sum[:, :2], vec_sum[:, 6:8], vec_sum[:, 2:3]],
+        + [own_rows(late_cols), own_rows(early_cols)[:, :1]],
         axis=1,
-    )
-    grad_feed = jnp.concatenate(
-        [join(up_mine, up_other), join(down_mine, down_other), vec_sum[:, 3:6]], axis=1
     )
     grad_up = join(bias_mine, bias_far).reshape(hidden)
 
     new_attn, new_attn_first, new_attn_second = adamw_step(
         attn_params, attn_first, attn_second, grad_attn
-    )
-    new_feed, new_feed_first, new_feed_second = adamw_step(
-        feed_params, feed_first, feed_second, grad_feed
     )
     new_up, new_up_first, new_up_second = adamw_step(
         up_bias, up_bias_first, up_bias_second, grad_up

time: 559 us -> 572 us (1.023)
  the two profiles are of different devices: /device:TPU:0 before, /device:TPU:9 now
where the time goes in v2:
time: 572 us; the launch traced here: 562 us
  waiting for transfers between devices  225 us (39%)
  matrix products  119 us (21%)
  starting transfers between devices  77.2 us (13%)
  other arithmetic  59.3 us (10%)
  local copies, waits for them, and re-layouts  42.7 us (7%)
  Pallas kernels  35.7 us (6%)
    ppermute x50, waiting for transfers between devices, dp_swap(): return lax.ppermute(value, 'dp', [(i, i ^ mask) for i in range(count)])  150 us
    ppermute x16, waiting for transfers between devices, y_swap(): return lax.ppermute(value, 'ctx', [(i, i ^ 1) for i in range(count)])  74.8 us
    ppermute x50, starting transfers between devices, dp_swap(): return lax.ppermute(value, 'dp', [(i, i ^ mask) for i in range(count)])  60.6 us
    dot_general x16, matrix products, mm_tn(): lax.dot_general(left, right, (((0,), (0,)), ((), ())), preferred_element_...  47.5 us
    dot_general x7, matrix products, mm(): return jnp.dot(left, right, preferred_element_type=f32)  43.7 us
    dot_general x8, matrix products, mm_nt(): lax.dot_general(left, right, (((1,), (1,)), ((), ())), preferred_element_...  28.2 us
    pallas_call x1, Pallas kernels, attend_back(): pl.pallas_call(back_kernel, grid=(images,), in_specs=[whole((seq, wide)),...  20.9 us
    ppermute x16, starting transfers between devices, y_swap(): return lax.ppermute(value, 'ctx', [(i, i ^ 1) for i in range(count)])  16.6 us
  transfers between devices with their start and end apart: 66, of which 29 were waited for; matrix products, arithmetic and copies ran while one was open for 28% of the time, Pallas kernels for 4%

profile of v2, /device:TPU:9, one launch (start us, length us, event | category | flops | bytes accessed | tf_op | source)
XLA Modules:
  0.0 561.7 jit_solution(1005387850358874789)
XLA Ops:
  16.3 10.1 %collective-permute-done.2 = bf16[72,2376]{1,0:T(8,128)(2,1)S(1)} collective-permute-done((bf16[72,2376]{1,0:T(8,128)(2,1)S(1)}, bf16[72,2376]{1,0:T(8,128)(2,1)S(1)}, u32[]{:S(2)}, u32[]{:S(2)}) %collective-permute-start.2) | collective-permute-done | bytes 342176 | tf_op jit(solution)/shard_map/ppermute | solution.py:72
  29.9 14.9 %collective-permute-done.4 = bf16[72,2376]{1,0:T(8,128)(2,1)S(1)} collective-permute-done((bf16[72,2376]{1,0:T(8,128)(2,1)S(1)}, bf16[72,2376]{1,0:T(8,128)(2,1)S(1)}, u32[]{:S(2)}, u32[]{:S(2)}) %collective-permute-start.4) | collective-permute-done | bytes 342176 | tf_op jit(solution)/shard_map/ppermute | solution.py:72
  47.6 8.1 %collective-permute-done.14 = bf16[72,2152]{1,0:T(8,128)(2,1)S(1)} collective-permute-done((bf16[72,2152]{1,0:T(8,128)(2,1)S(1)}, bf16[72,2152]{1,0:T(8,128)(2,1)S(1)}, u32[]{:S(2)}, u32[]{:S(2)}) %collective-permute-start.14) | collective-permute-done | bytes 309920 | tf_op jit(solution)/shard_map/ppermute | solution.py:72
  60.2 13.4 %collective-permute-done.16 = bf16[72,2152]{1,0:T(8,128)(2,1)S(1)} collective-permute-done((bf16[72,2152]{1,0:T(8,128)(2,1)S(1)}, bf16[72,2152]{1,0:T(8,128)(2,1)S(1)}, u32[]{:S(2)}, u32[]{:S(2)}) %collective-permute-start.16) | collective-permute-done | bytes 309920 | tf_op jit(solution)/shard_map/ppermute | solution.py:72
  89.6 15.6 %collective-permute-done.5 = bf16[288,2376]{1,0:T(8,128)(2,1)S(1)} collective-permute-done((bf16[288,2376]{1,0:T(8,128)(2,1)S(1)}, bf16[288,2376]{1,0:T(8,128)(2,1)S(1)}, u32[]{:S(2)}, u32[]{:S(2)}) %collective-permute-start.5) | collective-permute-done | bytes 1368608 | tf_op jit(solution)/shard_map/ppermute | solution.py:72
  108.3 12.1 %collective-permute-done.7 = bf16[144,2376]{1,0:T(8,128)(2,1)S(1)} collective-permute-done((bf16[144,2376]{1,0:T(8,128)(2,1)S(1)}, bf16[144,2376]{1,0:T(8,128)(2,1)S(1)}, u32[]{:S(2)}, u32[]{:S(2)}) %collective-permute-start.7) | collective-permute-done | bytes 684320 | tf_op jit(solution)/shard_map/ppermute | solution.py:89
  120.3 5.4 collective-permute-start.21
  137.2 23.0 %collective-permute-done.17 = bf16[288,2152]{1,0:T(8,128)(2,1)} collective-permute-done((bf16[288,2152]{1,0:T(8,128)(2,1)S(1)}, bf16[288,2152]{1,0:T(8,128)(2,1)}, u32[]{:S(2)}, u32[]{:S(2)}) %collective-permute-start.17) | collective-permute-done | bytes 1239584 | tf_op jit(solution)/shard_map/ppermute | solution.py:72
  164.9 12.3 %add_convert_fusion = bf16[1536,1792]{1,0:T(8,128)(2,1)} fusion(f32[1792]{0:T(1024)S(1)} %concatenate.177, bf16[1152,2376]{1,0:T(8,128)(2,1)} %copy-done.21, bf16[768,1152]{1,0:T(8,128)(2,1)} %collective-permute-done.9, bf16[768,1152]{1,0:T(8,128)(2,1)} %get-tuple-element.159), kind=kOutput, calls=%fused_computation | convolution fusion | flops 6354370560 | bytes 13179904 | tf_op jit(solution)/shard_map/dot_general | solution.py:59
  177.2 14.7 %shard_map.227 = (bf16[2,384,576]{2,1,0:T(8,128)(2,1)}, f32[2,8,384]{2,1,0:T(8,128)}) custom-call(bf16[2,768,1792]{2,1,0:T(8,128)(2,1)} %bitcast.68, f32[2,768,1]{2,1,0:T(8,128)} %copy.29.valid_ref), custom_call_target="tpu_custom_call" | custom-call | flops 1358954496 | bytes 5505024 | tf_op jit(solution)/shard_map/pallas_call | solution.py:191
  202.9 30.1 %collective-permute-done.19 = bf16[144,2152]{1,0:T(8,128)(2,1)S(1)} collective-permute-done((bf16[144,2152]{1,0:T(8,128)(2,1)S(1)}, bf16[144,2152]{1,0:T(8,128)(2,1)S(1)}, u32[]{:S(2)}, u32[]{:S(2)}) %collective-permute-start.19) | collective-permute-done | bytes 619808 | tf_op jit(solution)/shard_map/ppermute | solution.py:89
  242.2 5.7 %collective-permute-done.27 = bf16[144,2152]{1,0:T(8,128)(2,1)S(1)} collective-permute-done((bf16[144,2152]{1,0:T(8,128)(2,1)S(1)}, bf16[144,2152]{1,0:T(8,128)(2,1)S(1)}, u32[]{:S(2)}, u32[]{:S(2)}) %collective-permute-start.27) | collective-permute-done | bytes 619808 | tf_op jit(solution)/shard_map/ppermute | solution.py:89
  249.0 8.6 %multiply_convert_fusion = (bf16[768,2152]{0,1:T(8,128)(2,1)S(1)}, f32[768,2152]{0,1:T(8,128)}) fusion(f32[2152]{0:T(1024)S(1)} %slice_select_fusion.6, bf16[1152,2152]{1,0:T(8,128)(2,1)S(1)} %bitcast.62, bf16[384,1152]{1,0:T(8,128)(2,1)S(1)} %collective-permute-done.13, bf16[384,1152]{1,0:T(8,128)(2,1)S(1)} %add_convert_fusion.7), kind=kOutput, calls=%fused_computation.9 | convolution fusion | flops 3827970048 | bytes 16652704 | tf_op jit(solution)/shard_map/dot_general | solution.py:59
  269.4 11.9 %fusion.155 = (f32[2152]{0:T(1024)S(1)}, bf16[768,2152]{0,1:T(8,128)(2,1)S(1)}) fusion(f32[768,2152]{0,1:T(8,128)} %get-tuple-element.218, f32[2152]{0:T(1024)S(1)} %slice_select_fusion.6, bf16[768,1152]{1,0:T(8,128)(2,1)S(1)} %copy-done.14, bf16[1152,2152]{1,0:T(8,128)(2,1)S(1)} %constant_dynamic-update-slice_fusion.10), kind=kOutput, calls=%fused_computation.365 | convolution fusion | flops 3844261888 | bytes 16661312 | tf_op jit(solution)/shard_map/dot_general | solution.py:59
  308.5 11.7 %collective-permute-done.47 = f32[1,6760]{1,0:T(1,128)S(1)} collective-permute-done((f32[1,6760]{1,0:T(1,128)S(1)}, f32[1,6760]{1,0:T(1,128)S(1)}, u32[]{:S(2)}, u32[]{:S(2)}) %collective-permute-start.47) | collective-permute-done | bytes 27072 | tf_op jit(solution)/shard_map/ppermute | solution.py:89
  351.0 20.9 %shard_map.228 = (bf16[2,768,1792]{2,1,0:T(8,128)(2,1)}, f32[2,8,1792]{2,1,0:T(8,128)}) custom-call(bf16[2,768,1792]{2,1,0:T(8,128)(2,1)} %bitcast.69, f32[2,768,1]{2,1,0:T(8,128)} %copy.29.valid_ref, bf16[2,384,576]{2,1,0:T(8,128)(2,1)} %get-tuple-element.73.mixed_ref, f32[2,8,384]{2,1,0:T(8,128)} %get-tuple-element.78.log_ref, bf16[2,384,576]{2,1,0:T(8,128)(2,1)} %bitcast.54), custom_call_target="tpu_custom_call" | custom-call | flops 3397386240 | bytes 11010048 | tf_op jit(solution)/shard_map/pallas_call | solution.py:241
  372.0 5.3 collective-permute-done.60
  388.8 7.5 %fusion.13 = f32[1536,1152]{1,0:T(8,128)S(1)} fusion(bf16[1536,1792]{1,0:T(8,128)(2,1)S(1)} %bitcast.74, bf16[1152,2376]{1,0:T(8,128)(2,1)S(1)} %bitcast.58), kind=kOutput, calls=%fused_computation.35 | convolution fusion | flops 6341787648 | bytes 16711680 | tf_op jit(solution)/shard_map/dot_general | solution.py:63
  402.5 5.2 convolution_convert_fusion.9
  423.5 12.5 %collective-permute-done.34 = bf16[144,2368]{1,0:T(8,128)(2,1)S(1)} collective-permute-done((bf16[144,2368]{1,0:T(8,128)(2,1)S(1)}, bf16[144,2368]{1,0:T(8,128)(2,1)S(1)}, u32[]{:S(2)}, u32[]{:S(2)}) %collective-permute-start.34) | collective-permute-done | bytes 682016 | tf_op jit(solution)/shard_map/ppermute | solution.py:89
  442.1 8.7 %collective-permute-done.64 = bf16[72,2152]{1,0:T(8,128)(2,1)S(1)} collective-permute-done((bf16[72,2152]{1,0:T(8,128)(2,1)S(1)}, bf16[72,2152]{1,0:T(8,128)(2,1)S(1)}, u32[]{:S(2)}, u32[]{:S(2)}) %collective-permute-start.64) | collective-permute-done | bytes 309920 | tf_op jit(solution)/shard_map/ppermute | solution.py:72
  456.2 13.0 %collective-permute-done.56 = bf16[72,2152]{1,0:T(8,128)(2,1)S(1)} collective-permute-done((bf16[72,2152]{1,0:T(8,128)(2,1)}, bf16[72,2152]{1,0:T(8,128)(2,1)S(1)}, u32[]{:S(2)}, u32[]{:S(2)}) %collective-permute-start.56) | collective-permute-done | bytes 309920 | tf_op jit(solution)/shard_map/ppermute | solution.py:72
  469.2 8.5 %collective-permute-done.57 = bf16[72,2152]{1,0:T(8,128)(2,1)S(1)} collective-permute-done((bf16[72,2152]{1,0:T(8,128)(2,1)S(1)}, bf16[72,2152]{1,0:T(8,128)(2,1)S(1)}, u32[]{:S(2)}, u32[]{:S(2)}) %collective-permute-start.57) | collective-permute-done | bytes 309920 | tf_op jit(solution)/shard_map/ppermute | solution.py:72
  493.3 9.9 %collective-permute-done.44 = f32[1,4608]{1,0:T(1,128)S(1)} collective-permute-done((f32[1,4608]{1,0:T(1,128)S(1)}, f32[1,4608]{1,0:T(1,128)S(1)}, u32[]{:S(2)}, u32[]{:S(2)}) %collective-permute-start.44) | collective-permute-done | bytes 18464 | tf_op jit(solution)/shard_map/ppermute | solution.py:72
  (406 shorter events, 270.3 us)
Async XLA Ops:
  14.9 61.4 %collective-permute-start.1 = (bf16[384,1152]{1,0:T(8,128)(2,1)S(1)}, bf16[384,1152]{1,0:T(8,128)(2,1)S(1)}, u32[]{:S(2)}, u32[]{:S(2)}) collective-permute-start(bf16[384,1152]{1,0:T(8,128)(2,1)S(1)} %bitcast.55), channel_id=1, source_target_pairs={{0,1},{1,0},{2,3},{3,2},{4,5},{5,4},{6,7},{7,6},{8,9},{9,8},{10,11... | collective-permute-start | bytes 2654216 | tf_op jit(solution)/shard_map/ppermute | solution.py:89
  73.5 57.7 %collective-permute-start.22 = (bf16[72,2152]{1,0:T(8,128)(2,1)S(1)}, bf16[72,2152]{1,0:T(8,128)(2,1)S(1)}, u32[]{:S(2)}, u32[]{:S(2)}) collective-permute-start(bf16[72,2152]{1,0:T(8,128)(2,1)S(1)} %get-tuple-element.80), channel_id=1, source_target_pairs={{0,8},{2,10},{4,12},{6,14},{8,0},{10,2},{12,4},{14,6},{16,24},{18,... | collective-permute-start | bytes 929672 | tf_op jit(solution)/shard_map/ppermute | solution.py:72
  73.5 57.7 %collective-permute-start.23 = (bf16[72,2152]{1,0:T(8,128)(2,1)S(1)}, bf16[72,2152]{1,0:T(8,128)(2,1)S(1)}, u32[]{:S(2)}, u32[]{:S(2)}) collective-permute-start(bf16[72,2152]{1,0:T(8,128)(2,1)S(1)} %get-tuple-element.80), channel_id=1, source_target_pairs={{0,16},{2,18},{4,20},{6,22},{8,24},{10,26},{12,28},{14,30},{16,0},... | collective-permute-start | bytes 929672 | tf_op jit(solution)/shard_map/ppermute | solution.py:72
  76.0 55.3 %collective-permute-start.24 = (bf16[72,2152]{1,0:T(8,128)(2,1)S(1)}, bf16[72,2152]{1,0:T(8,128)(2,1)S(1)}, u32[]{:S(2)}, u32[]{:S(2)}) collective-permute-start(bf16[72,2152]{1,0:T(8,128)(2,1)S(1)} %get-tuple-element.80), channel_id=1, source_target_pairs={{0,24},{2,26},{4,28},{6,30},{8,16},{10,18},{12,20},{14,22},{16,8},... | collective-permute-start | bytes 929672 | tf_op jit(solution)/shard_map/ppermute | solution.py:72
  131.2 33.6 %collective-permute-start.9 = (bf16[768,1152]{1,0:T(8,128)(2,1)}, bf16[768,1152]{1,0:T(8,128)(2,1)}, u32[]{:S(2)}, u32[]{:S(2)}) collective-permute-start(bf16[768,1152]{1,0:T(8,128)(2,1)} %get-tuple-element.159), channel_id=1, source_target_pairs={{0,2},{2,0},{4,6},{6,4},{8,10},{10,8},{12,14},{14,12},{16,18},{18,... | collective-permute-start | bytes 5308424 | tf_op jit(solution)/shard_map/ppermute | solution.py:72
  191.9 42.9 %collective-permute-start.25 = (bf16[288,2152]{1,0:T(8,128)(2,1)S(1)}, bf16[288,2152]{1,0:T(8,128)(2,1)S(1)}, u32[]{:S(2)}, u32[]{:S(2)}) collective-permute-start(bf16[288,2152]{1,0:T(8,128)(2,1)S(1)} %pad_maximum_fusion.19), channel_id=1, source_target_pairs={{0,4},{2,6},{4,0},{6,2},{8,12},{10,14},{12,8},{14,10},{16,20},{18,... | collective-permute-start | bytes 3718664 | tf_op jit(solution)/shard_map/ppermute | solution.py:72
  192.4 42.5 %collective-permute-start.26 = (bf16[288,2152]{1,0:T(8,128)(2,1)S(1)}, bf16[288,2152]{1,0:T(8,128)(2,1)S(1)}, u32[]{:S(2)}, u32[]{:S(2)}) collective-permute-start(bf16[288,2152]{1,0:T(8,128)(2,1)S(1)} %pad_maximum_fusion.19), channel_id=1, source_target_pairs={{0,1},{1,0},{2,3},{3,2},{4,5},{5,4},{6,7},{7,6},{8,9},{9,8},{10,11... | collective-permute-start | bytes 3718664 | tf_op jit(solution)/shard_map/ppermute | solution.py:89
  197.1 40.6 %collective-permute-start.12 = (f32[384,1152]{1,0:T(8,128)S(1)}, f32[384,1152]{1,0:T(8,128)S(1)}, u32[]{:S(2)}, u32[]{:S(2)}) collective-permute-start(f32[384,1152]{1,0:T(8,128)S(1)} %slice.523), channel_id=1, source_target_pairs={{0,2},{2,0},{4,6},{6,4},{8,10},{10,8},{12,14},{14,12},{16,18},{18,... | collective-permute-start | bytes 5308424 | tf_op jit(solution)/shard_map/ppermute | solution.py:72
  199.4 33.6 %collective-permute-start.19 = (bf16[144,2152]{1,0:T(8,128)(2,1)S(1)}, bf16[144,2152]{1,0:T(8,128)(2,1)S(1)}, u32[]{:S(2)}, u32[]{:S(2)}) collective-permute-start(bf16[144,2152]{1,0:T(8,128)(2,1)S(1)} %slice.529), channel_id=1, source_target_pairs={{0,1},{1,0},{2,3},{3,2},{4,5},{5,4},{6,7},{7,6},{8,9},{9,8},{10,11... | collective-permute-start | bytes 1859336 | tf_op jit(solution)/shard_map/ppermute | solution.py:89
  293.4 37.7 %collective-permute-start.53 = (bf16[288,2152]{1,0:T(8,128)(2,1)}, bf16[288,2152]{1,0:T(8,128)(2,1)}, u32[]{:S(2)}, u32[]{:S(2)}) collective-permute-start(bf16[288,2152]{1,0:T(8,128)(2,1)} %convolution_convert_fusion), channel_id=1, source_target_pairs={{0,4},{2,6},{4,0},{6,2},{8,12},{10,14},{12,8},{14,10},{16,20},{18,... | collective-permute-start | bytes 3718664 | tf_op jit(solution)/shard_map/ppermute | solution.py:72
  322.2 49.8 %collective-permute-start.61 = (bf16[288,2152]{1,0:T(8,128)(2,1)}, bf16[288,2152]{1,0:T(8,128)(2,1)}, u32[]{:S(2)}, u32[]{:S(2)}) collective-permute-start(bf16[288,2152]{1,0:T(8,128)(2,1)} %convolution_convert_fusion.4), channel_id=1, source_target_pairs={{0,1},{1,0},{2,3},{3,2},{4,5},{5,4},{6,7},{7,6},{8,9},{9,8},{10,11... | collective-permute-start | bytes 3718664 | tf_op jit(solution)/shard_map/ppermute | solution.py:89
  322.4 96.3 %collective-permute-start.52 = (bf16[288,2152]{1,0:T(8,128)(2,1)}, bf16[288,2152]{1,0:T(8,128)(2,1)}, u32[]{:S(2)}, u32[]{:S(2)}) collective-permute-start(bf16[288,2152]{1,0:T(8,128)(2,1)} %convolution_convert_fusion.2), channel_id=1, source_target_pairs={{0,4},{2,6},{4,0},{6,2},{8,12},{10,14},{12,8},{14,10},{16,20},{18,... | collective-permute-start | bytes 3718664 | tf_op jit(solution)/shard_map/ppermute | solution.py:72
  328.7 48.6 %collective-permute-start.60 = (bf16[288,2152]{1,0:T(8,128)(2,1)}, bf16[288,2152]{1,0:T(8,128)(2,1)}, u32[]{:S(2)}, u32[]{:S(2)}) collective-permute-start(bf16[288,2152]{1,0:T(8,128)(2,1)} %add_convert_fusion.4), channel_id=1, source_target_pairs={{0,4},{2,6},{4,0},{6,2},{8,12},{10,14},{12,8},{14,10},{16,20},{18,... | collective-permute-start | bytes 3718664 | tf_op jit(solution)/shard_map/ppermute | solution.py:72
  339.7 80.3 %collective-permute-start.54 = (bf16[288,2152]{1,0:T(8,128)(2,1)}, bf16[288,2152]{1,0:T(8,128)(2,1)}, u32[]{:S(2)}, u32[]{:S(2)}) collective-permute-start(bf16[288,2152]{1,0:T(8,128)(2,1)} %add_convert_fusion.6), channel_id=1, source_target_pairs={{0,1},{1,0},{2,3},{3,2},{4,5},{5,4},{6,7},{7,6},{8,9},{9,8},{10,11... | collective-permute-start | bytes 3718664 | tf_op jit(solution)/shard_map/ppermute | solution.py:89
  379.7 60.9 %collective-permute-start.62 = (bf16[72,2152]{1,0:T(8,128)(2,1)S(1)}, bf16[72,2152]{1,0:T(8,128)(2,1)S(1)}, u32[]{:S(2)}, u32[]{:S(2)}) collective-permute-start(bf16[72,2152]{1,0:T(8,128)(2,1)S(1)} %get-tuple-element.176), channel_id=1, source_target_pairs={{0,8},{2,10},{4,12},{6,14},{8,0},{10,2},{12,4},{14,6},{16,24},{18,... | collective-permute-start | bytes 929672 | tf_op jit(solution)/shard_map/ppermute | solution.py:72
  381.1 60.1 %collective-permute-start.63 = (bf16[72,2152]{1,0:T(8,128)(2,1)S(1)}, bf16[72,2152]{1,0:T(8,128)(2,1)S(1)}, u32[]{:S(2)}, u32[]{:S(2)}) collective-permute-start(bf16[72,2152]{1,0:T(8,128)(2,1)S(1)} %get-tuple-element.175), channel_id=1, source_target_pairs={{0,16},{2,18},{4,20},{6,22},{8,24},{10,26},{12,28},{14,30},{16,0},... | collective-permute-start | bytes 929672 | tf_op jit(solution)/shard_map/ppermute | solution.py:72
  396.6 42.6 %collective-permute-start.31 = (f32[768,1152]{1,0:T(8,128)S(1)}, f32[768,1152]{1,0:T(8,128)S(1)}, u32[]{:S(2)}, u32[]{:S(2)}) collective-permute-start(f32[768,1152]{1,0:T(8,128)S(1)} %slice.568), channel_id=1, source_target_pairs={{0,2},{2,0},{4,6},{6,4},{8,10},{10,8},{12,14},{14,12},{16,18},{18,... | collective-permute-start | bytes 10616840 | tf_op jit(solution)/shard_map/ppermute | solution.py:72
  440.6 37.1 %collective-permute-start.57 = (bf16[72,2152]{1,0:T(8,128)(2,1)S(1)}, bf16[72,2152]{1,0:T(8,128)(2,1)S(1)}, u32[]{:S(2)}, u32[]{:S(2)}) collective-permute-start(bf16[72,2152]{1,0:T(8,128)(2,1)S(1)} %copy-done.23), channel_id=1, source_target_pairs={{0,24},{2,26},{4,28},{6,30},{8,16},{10,18},{12,20},{14,22},{16,8},... | collective-permute-start | bytes 929672 | tf_op jit(solution)/shard_map/ppermute | solution.py:72
  441.3 42.4 %collective-permute-start.37 = (bf16[288,2368]{1,0:T(8,128)(2,1)S(1)}, bf16[288,2368]{1,0:T(8,128)(2,1)S(1)}, u32[]{:S(2)}, u32[]{:S(2)}) collective-permute-start(bf16[288,2368]{1,0:T(8,128)(2,1)S(1)} %pad_maximum_fusion.16), channel_id=1, source_target_pairs={{0,1},{1,0},{2,3},{3,2},{4,5},{5,4},{6,7},{7,6},{8,9},{9,8},{10,11... | collective-permute-start | bytes 4091912 | tf_op jit(solution)/shard_map/ppermute | solution.py:89
  450.8 32.9 %collective-permute-start.36 = (bf16[288,2368]{1,0:T(8,128)(2,1)S(1)}, bf16[288,2368]{1,0:T(8,128)(2,1)S(1)}, u32[]{:S(2)}, u32[]{:S(2)}) collective-permute-start(bf16[288,2368]{1,0:T(8,128)(2,1)S(1)} %pad_maximum_fusion.15), channel_id=1, source_target_pairs={{0,4},{2,6},{4,0},{6,2},{8,12},{10,14},{12,8},{14,10},{16,20},{18,... | collective-permute-start | bytes 4091912 | tf_op jit(solution)/shard_map/ppermute | solution.py:72
  453.5 65.1 %collective-permute-start.65 = (f32[36,2152]{1,0:T(8,128)}, f32[36,2152]{1,0:T(8,128)}, u32[]{:S(2)}, u32[]{:S(2)}) collective-permute-start(f32[36,2152]{1,0:T(8,128)} %get-tuple-element.191), channel_id=1, source_target_pairs={{0,2},{2,0},{4,6},{6,4},{8,10},{10,8},{12,14},{14,12},{16,18},{18,... | collective-permute-start | bytes 929672 | tf_op jit(solution)/shard_map/ppermute | solution.py:72
  478.7 43.7 %collective-permute-start.58 = (f32[36,2152]{1,0:T(8,128)}, f32[36,2152]{1,0:T(8,128)}, u32[]{:S(2)}, u32[]{:S(2)}) collective-permute-start(f32[36,2152]{1,0:T(8,128)} %get-tuple-element.193), channel_id=1, source_target_pairs={{0,2},{2,0},{4,6},{6,4},{8,10},{10,8},{12,14},{14,12},{16,18},{18,... | collective-permute-start | bytes 929672 | tf_op jit(solution)/shard_map/ppermute | solution.py:72
  486.7 41.2 %collective-permute-start.38 = (bf16[72,2368]{1,0:T(8,128)(2,1)}, bf16[72,2368]{1,0:T(8,128)(2,1)}, u32[]{:S(2)}, u32[]{:S(2)}) collective-permute-start(bf16[72,2368]{1,0:T(8,128)(2,1)} %get-tuple-element.170), channel_id=1, source_target_pairs={{0,8},{2,10},{4,12},{6,14},{8,0},{10,2},{12,4},{14,6},{16,24},{18,... | collective-permute-start | bytes 1022984 | tf_op jit(solution)/shard_map/ppermute | solution.py:72
  486.7 41.2 %collective-permute-start.39 = (bf16[72,2368]{1,0:T(8,128)(2,1)}, bf16[72,2368]{1,0:T(8,128)(2,1)}, u32[]{:S(2)}, u32[]{:S(2)}) collective-permute-start(bf16[72,2368]{1,0:T(8,128)(2,1)} %get-tuple-element.169), channel_id=1, source_target_pairs={{0,16},{2,18},{4,20},{6,22},{8,24},{10,26},{12,28},{14,30},{16,0},... | collective-permute-start | bytes 1022984 | tf_op jit(solution)/shard_map/ppermute | solution.py:72
  (91 other events, 1390.9 us)

commit v3 on v2

--- a/solution.py
+++ b/solution.py
@@ -23,8 +23,14 @@
 f32 = jnp.float32
 
 
-def gelu_tanh(values):
-    return jax.nn.gelu(values, approximate=True)
+def gelu_pair(values):
+    root = math.sqrt(2.0 / math.pi)
+    square = values * values
+    bent = jnp.tanh(root * (values + 0.044715 * (square * values)))
+    value = 0.5 * values * (1.0 + bent)
+    inner = root * (1.0 + (3.0 * 0.044715) * square)
+    slope = 0.5 * (1.0 + bent) + 0.5 * values * ((1.0 - bent * bent) * inner)
+    return value, slope
 
 
 def norm_stats(values):
@@ -288,20 +294,24 @@
     attn_half = attn_params.astype(bf16)
     feed_half = feed_params.astype(bf16)
 
-    fill = -3 * half_w % 128
+    vecs = attn_params.shape[1] - 4 * width + feed_params.shape[1] - 2 * hidden
+    fill = -(3 * half_w + vecs) % 128 + vecs
     packed_w = 3 * half_w + fill
 
     def pick(at):
-        parts = [
+        halves = [
             attn_half[:, i * width + at * half_w : i * width + (at + 1) * half_w]
             for i in range(4)
         ]
-        parts.insert(3, jnp.zeros((owned, fill), bf16))
-        parts.append(attn_half[:, 4 * width :])
-        parts.append(feed_half[:, 2 * hidden :])
-        for i in range(2):
-            parts.append(feed_half[:, i * hidden + at * half_h : i * hidden + (at + 1) * half_h])
-        return jnp.concatenate(parts, axis=1)
+        feeds = [
+            feed_half[:, i * hidden + at * half_h : i * hidden + (at + 1) * half_h]
+            for i in range(2)
+        ]
+        vectors = [attn_half[:, 4 * width :], feed_half[:, 2 * hidden :]]
+        gap = [jnp.zeros((owned, fill - vecs), bf16)]
+        return jnp.concatenate(
+            halves[:3] + vectors + gap + [feeds[0], halves[3], feeds[1]], axis=1
+        )
 
     part_zero, part_one = pick(0), pick(1)
     keep = jnp.where(first_core, part_zero, part_one)
@@ -310,16 +320,15 @@
     shard = jnp.concatenate(
         [jnp.where(first_core, keep, got), jnp.where(first_core, got, keep)], axis=0
     )
-    vecs = attn_params.shape[1] - 4 * width + feed_params.shape[1] - 2 * hidden
-    cut = packed_w + half_w + vecs
-    line_a = gather_line(shard[:, :cut], depth)
+    cut_c = packed_w + half_h + half_w
+    line_a = gather_line(shard[:, :packed_w], depth)
     rows_far = y_swap(after(rows_own, shard))
     sides_a = gather_sides(line_a, rows_far)
     all_a = gather_corner(sides_a)
     w_attn = gather_all(all_a)
-    line_c = gather_line(after(shard[:, cut : cut + half_h], *line_a), depth)
+    line_c = gather_line(after(shard[:, packed_w:cut_c], *line_a), depth)
     sides_c = gather_sides(line_c, *sides_a[1:])
-    line_d = gather_line(after(shard[:, cut + half_h :], *line_c), depth)
+    line_d = gather_line(after(shard[:, cut_c:], *line_c), depth)
 
     block = 2 * owned
     spot = after(jnp.arange(width, dtype=jnp.int32), shard)
@@ -341,9 +350,8 @@
         return both[: values.shape[0]] + both[values.shape[0] :]
 
 
-    w_qkv = w_attn[:, :packed_w]
-    w_o = w_attn[:, packed_w : packed_w + half_w]
-    vec = w_attn[:, packed_w + half_w :]
+    w_qkv = w_attn
+    vec = w_attn[:, 3 * half_w : 3 * half_w + vecs]
     vec_nat = mm(order, vec[:, 2:4])
     vec_t = vec.astype(f32).T
     gain_one, shift_one, bias_o = vec_t[0], vec_t[1], vec_t[4]
@@ -375,10 +383,11 @@
         return (mm(left, right) + bias_qkv).astype(bf16)
 
     packed = project(one_all, w_qkv).reshape(2, seq, packed_w)
+    all_c = gather_corner(sides_c, packed)
+    sides_d = gather_sides(line_d, packed, *sides_c[1:])
     mixed, log_total = attend(packed, valid, local_len, half_w)
-    all_c = gather_corner(sides_c, mixed)
-    w_up = gather_all(all_c)
-    sides_d = gather_sides(line_d, mixed, *sides_c[1:])
+    w_up = gather_all([piece[:, :half_h] for piece in all_c])
+    w_o = gather_all([piece[:, half_h:] for piece in all_c])
     mixed_rows = mixed.reshape(2 * local_len, half_w)
     part = mm_nt(mixed_rows, w_o)
     resid = rows_in + part[:local_len] + core_swap(part[local_len:]) + bias_o
@@ -391,20 +400,21 @@
 
     def activate(left, right):
         values = mm(left, right) + bias_up
-        return values, gelu_tanh(values).astype(bf16)
-
-    pre_act, act_half = activate(two_both, w_up)
+        value, slope = gelu_pair(values)
+        return slope.astype(bf16), value.astype(bf16)
+
+    slope_half, act_half = activate(two_both, w_up)
     down_last = weight_corner(grad_both, act_half)
     down_chunks = weight_chunks(grad_both, act_half)
     down_last, down_chunks = after((down_last, down_chunks), *sides_d[1:])
-    down_corner = scatter_corner(down_last, 2)
+    down_corner = scatter_corner(down_last, 1)
 
     def activate_back(left, right):
-        values = jax.vjp(gelu_tanh, pre_act)[1](mm(left, right))[0]
+        values = mm(left, right) * slope_half.astype(f32)
         return values, values.astype(bf16)
 
     grad_pre, grad_pre_half = activate_back(after(grad_both, *down_chunks), w_down)
-    up_corner = scatter_corner(weight_corner(two_both, grad_pre_half), 0)
+    up_corner = scatter_corner(weight_corner(two_both, grad_pre_half), 1)
     part = mm_nt(grad_pre_half, w_up)
     part_far = core_swap(part[local_len:])
     up_chunks = weight_chunks(two_both, after(grad_pre_half, part))

time: 572 us -> 591 us (1.033)
  waiting for transfers between devices: 225 us -> 238 us
    ppermute x16 -> x17, waiting for transfers between devices: 74.8 us -> 99.6 us  [y_swap(): return lax.ppermute(value, 'ctx', [(i, i ^ 1) for i in range(count)])]
    ppermute x50 -> x51, waiting for transfers between devices: 150 us -> 138 us  [dp_swap(): return lax.ppermute(value, 'dp', [(i, i ^ mask) for i in range(count)])]
    dot_general x16, matrix products: 47.5 us -> 40.5 us  [mm_tn(): lax.dot_general(left, right, (((0,), (0,)), ((), ())), preferred_element_...]
    ppermute x50 -> x51, starting transfers between devices: 60.6 us -> 67.3 us  [dp_swap(): return lax.ppermute(value, 'dp', [(i, i ^ mask) for i in range(count)])]
    unnamed x115 -> x139, local copies, waits for them, and re-layouts: 16.1 us -> 22 us
    ppermute x16 -> x17, starting transfers between devices: 16.6 us -> 15.7 us  [y_swap(): return lax.ppermute(value, 'ctx', [(i, i ^ 1) for i in range(count)])]
  transfers between devices with their start and end apart: 66 -> 68, of which waited for: 29 -> 27; matrix products, arithmetic and copies ran while one was open for 28% -> 27% of each run, Pallas kernels for 4% -> 6%
where the time goes in v3:
time: 591 us; the launch traced here: 580 us
  waiting for transfers between devices  238 us (40%)
  matrix products  115 us (19%)
  starting transfers between devices  82.9 us (14%)
  other arithmetic  58.7 us (10%)
  local copies, waits for them, and re-layouts  48.3 us (8%)
  Pallas kernels  35.4 us (6%)
    ppermute x51, waiting for transfers between devices, dp_swap(): return lax.ppermute(value, 'dp', [(i, i ^ mask) for i in range(count)])  138 us
    ppermute x17, waiting for transfers between devices, y_swap(): return lax.ppermute(value, 'ctx', [(i, i ^ 1) for i in range(count)])  99.6 us
    ppermute x51, starting transfers between devices, dp_swap(): return lax.ppermute(value, 'dp', [(i, i ^ mask) for i in range(count)])  67.3 us
    dot_general x7, matrix products, mm(): return jnp.dot(left, right, preferred_element_type=f32)  41.6 us
    dot_general x16, matrix products, mm_tn(): lax.dot_general(left, right, (((0,), (0,)), ((), ())), preferred_element_...  40.5 us
    dot_general x8, matrix products, mm_nt(): lax.dot_general(left, right, (((1,), (1,)), ((), ())), preferred_element_...  32.5 us
    unnamed x139, local copies, waits for them, and re-layouts  22 us
    pallas_call x1, Pallas kernels, attend_back(): pl.pallas_call(back_kernel, grid=(images,), in_specs=[whole((seq, wide)),...  20.5 us
  transfers between devices with their start and end apart: 68, of which 27 were waited for; matrix products, arithmetic and copies ran while one was open for 27% of the time, Pallas kernels for 6%

profile of v3, /device:TPU:9, one launch (start us, length us, event | category | flops | bytes accessed | tf_op | source)
XLA Modules:
  0.0 580.3 jit_solution(14725913081192456790)
XLA Ops:
  15.8 6.4 %collective-permute-done.2 = bf16[72,1792]{1,0:T(8,128)(2,1)S(1)} collective-permute-done((bf16[72,1792]{1,0:T(8,128)(2,1)S(1)}, bf16[72,1792]{1,0:T(8,128)(2,1)S(1)}, u32[]{:S(2)}, u32[]{:S(2)}) %collective-permute-start.2) | collective-permute-done | bytes 258080 | tf_op jit(solution)/shard_map/ppermute | solution.py:78
  25.8 11.0 %collective-permute-done.4 = bf16[72,1792]{1,0:T(8,128)(2,1)S(1)} collective-permute-done((bf16[72,1792]{1,0:T(8,128)(2,1)S(1)}, bf16[72,1792]{1,0:T(8,128)(2,1)S(1)}, u32[]{:S(2)}, u32[]{:S(2)}) %collective-permute-start.4) | collective-permute-done | bytes 258080 | tf_op jit(solution)/shard_map/ppermute | solution.py:78
  39.6 12.4 %collective-permute-done.12 = bf16[72,2728]{1,0:T(8,128)(2,1)S(1)} collective-permute-done((bf16[72,2728]{1,0:T(8,128)(2,1)S(1)}, bf16[72,2728]{1,0:T(8,128)(2,1)S(1)}, u32[]{:S(2)}, u32[]{:S(2)}) %collective-permute-start.12) | collective-permute-done | bytes 392864 | tf_op jit(solution)/shard_map/ppermute | solution.py:78
  56.0 17.3 %collective-permute-done.14 = bf16[72,2728]{1,0:T(8,128)(2,1)S(1)} collective-permute-done((bf16[72,2728]{1,0:T(8,128)(2,1)S(1)}, bf16[72,2728]{1,0:T(8,128)(2,1)S(1)}, u32[]{:S(2)}, u32[]{:S(2)}) %collective-permute-start.14) | collective-permute-done | bytes 392864 | tf_op jit(solution)/shard_map/ppermute | solution.py:78
  90.8 10.1 %collective-permute-done.24 = bf16[72,2152]{1,0:T(8,128)(2,1)S(1)} collective-permute-done((bf16[72,2152]{1,0:T(8,128)(2,1)S(1)}, bf16[72,2152]{1,0:T(8,128)(2,1)S(1)}, u32[]{:S(2)}, u32[]{:S(2)}) %collective-permute-start.24) | collective-permute-done | bytes 309920 | tf_op jit(solution)/shard_map/ppermute | solution.py:78
  103.6 10.3 %collective-permute-done.6 = bf16[288,1792]{1,0:T(8,128)(2,1)S(1)} collective-permute-done((bf16[288,1792]{1,0:T(8,128)(2,1)S(1)}, bf16[288,1792]{1,0:T(8,128)(2,1)S(1)}, u32[]{:S(2)}, u32[]{:S(2)}) %collective-permute-start.6) | collective-permute-done | bytes 1032224 | tf_op jit(solution)/shard_map/ppermute | solution.py:95
  119.1 41.9 %collective-permute-done.7 = bf16[144,1792]{1,0:T(8,128)(2,1)S(1)} collective-permute-done((bf16[144,1792]{1,0:T(8,128)(2,1)S(1)}, bf16[144,1792]{1,0:T(8,128)(2,1)S(1)}, u32[]{:S(2)}, u32[]{:S(2)}) %collective-permute-start.7) | collective-permute-done | bytes 516128 | tf_op jit(solution)/shard_map/ppermute | solution.py:95
  177.7 9.8 %add_convert_fusion = bf16[1536,1792]{1,0:T(8,128)(2,1)} fusion(bf16[1152,1792]{1,0:T(8,128)(2,1)S(1)} %copy-done.26, f32[1792]{0:T(1024)S(1)} %concatenate.191, bf16[768,1152]{1,0:T(8,128)(2,1)} %collective-permute-done.9, bf16[768,1152]{1,0:T(8,128)(2,1)S(1)} %get-tuple-element.161), kind=kOutput, calls=%fused_computation | convolution fusion | flops 6354370560 | bytes 13179904 | tf_op jit(solution)/shard_map/dot_general | solution.py:65
  194.2 14.9 %shard_map.227 = (bf16[2,384,576]{2,1,0:T(8,128)(2,1)}, f32[2,8,384]{2,1,0:T(8,128)}) custom-call(bf16[2,768,1792]{2,1,0:T(8,128)(2,1)} %bitcast.72, f32[2,768,1]{2,1,0:T(8,128)} %copy.29.valid_ref), custom_call_target="tpu_custom_call" | custom-call | flops 1358954496 | bytes 5505024 | tf_op jit(solution)/shard_map/pallas_call | solution.py:197
  215.8 21.0 %collective-permute-done.25 = bf16[288,2152]{1,0:T(8,128)(2,1)S(1)} collective-permute-done((bf16[288,2152]{1,0:T(8,128)(2,1)S(1)}, bf16[288,2152]{1,0:T(8,128)(2,1)S(1)}, u32[]{:S(2)}, u32[]{:S(2)}) %collective-permute-start.25) | collective-permute-done | bytes 1239584 | tf_op jit(solution)/shard_map/ppermute | solution.py:78
  241.6 9.9 %collective-permute-done.27 = bf16[144,2152]{1,0:T(8,128)(2,1)S(1)} collective-permute-done((bf16[144,2152]{1,0:T(8,128)(2,1)S(1)}, bf16[144,2152]{1,0:T(8,128)(2,1)S(1)}, u32[]{:S(2)}, u32[]{:S(2)}) %collective-permute-start.27) | collective-permute-done | bytes 619808 | tf_op jit(solution)/shard_map/ppermute | solution.py:95
  253.9 8.7 %multiply_convert_fusion = (bf16[768,2152]{0,1:T(8,128)(2,1)S(1)}, f32[768,2152]{0,1:T(8,128)}) fusion(f32[2152]{0:T(1024)S(1)} %copy-done.38, bf16[1152,2152]{1,0:T(8,128)(2,1)S(1)} %slice_dynamic-update-slice_fusion.3, bf16[384,1152]{1,0:T(8,128)(2,1)S(1)} %collective-permute-done.20, bf16[384,1152]{1,0:T(8,128)(2,1)S(1)} %add_convert_fusion.5), kind=kOutput, calls=%fused_computation.14 | convolution fusion | flops 3827970048 | bytes 16652704 | tf_op jit(solution)/shard_map/dot_general | solution.py:65
  274.8 12.1 %fusion.158 = (f32[2152]{0:T(1024)S(1)}, bf16[768,2152]{0,1:T(8,128)(2,1)}) fusion(f32[768,2152]{0,1:T(8,128)} %get-tuple-element.225, f32[2152]{0:T(1024)S(1)} %copy-done.38, bf16[768,1152]{1,0:T(8,128)(2,1)S(1)} %copy-done.19, bf16[1152,2152]{1,0:T(8,128)(2,1)S(1)} %bitcast.64), kind=kOutput, calls=%fused_computation.378 | convolution fusion | flops 3844261888 | bytes 16661312 | tf_op jit(solution)/shard_map/dot_general | solution.py:65
  286.9 6.7 %fusion.172 = f32[768,1152]{1,0:T(8,128)S(1)} fusion(bf16[768,2152]{0,1:T(8,128)(2,1)} %get-tuple-element.90, bf16[1152,2152]{1,0:T(8,128)(2,1)S(1)} %slice_dynamic-update-slice_fusion.3), kind=kOutput, calls=%fused_computation.392 | convolution fusion | flops 3807903744 | bytes 11802624 | tf_op jit(solution)/shard_map/dot_general | solution.py:69
  317.4 6.0 %collective-permute-start.30 = (bf16[384,1152]{1,0:T(8,128)(2,1)}, bf16[384,1152]{1,0:T(8,128)(2,1)}, u32[]{:S(2)}, u32[]{:S(2)}) collective-permute-start(bf16[384,1152]{1,0:T(8,128)(2,1)} %convert_element_type.277), channel_id=1, source_target_pairs={{0,2},{2,0},{4,6},{6,4},{8,10},{10,8},{12,14},{14,12},{16,18},{18,... | collective-permute-start | bytes 2654216 | tf_op jit(solution)/shard_map/ppermute | solution.py:78
  326.0 22.4 %collective-permute-done.47 = f32[1,6760]{1,0:T(1,128)S(1)} collective-permute-done((f32[1,6760]{1,0:T(1,128)S(1)}, f32[1,6760]{1,0:T(1,128)S(1)}, u32[]{:S(2)}, u32[]{:S(2)}) %collective-permute-start.47) | collective-permute-done | bytes 27072 | tf_op jit(solution)/shard_map/ppermute | solution.py:95
  358.6 6.0 %collective-permute-start.51 = (f32[1,6760]{1,0:T(1,128)S(1)}, f32[1,6760]{1,0:T(1,128)S(1)}, u32[]{:S(2)}, u32[]{:S(2)}) collective-permute-start(f32[1,6760]{1,0:T(1,128)S(1)} %add.398), channel_id=1, source_target_pairs={{0,2},{2,0},{4,6},{6,4},{8,10},{10,8},{12,14},{14,12},{16,18},{18,... | collective-permute-start | bytes 81128 | tf_op jit(solution)/shard_map/ppermute | solution.py:78
  377.1 20.5 %shard_map.228 = (bf16[2,768,1792]{2,1,0:T(8,128)(2,1)}, f32[2,8,1792]{2,1,0:T(8,128)}) custom-call(bf16[2,768,1792]{2,1,0:T(8,128)(2,1)} %bitcast.73, f32[2,768,1]{2,1,0:T(8,128)} %copy.29.valid_ref, bf16[2,384,576]{2,1,0:T(8,128)(2,1)} %get-tuple-element.75.mixed_ref, f32[2,8,384]{2,1,0:T(8,128)} %get-tuple-element.80.log_ref, bf16[2,384,576]{2,1,0:T(8,128)(2,1)} %bitcast.58), custom_call_target="tpu_custom_call" | custom-call | flops 3397386240 | bytes 11010048 | tf_op jit(solution)/shard_map/pallas_call | solution.py:247
  407.7 9.5 %fusion.173 = f32[1536,1152]{1,0:T(8,128)S(1)} fusion(bf16[1536,1792]{1,0:T(8,128)(2,1)} %bitcast.74, bf16[1152,1792]{1,0:T(8,128)(2,1)S(1)} %copy-done.27), kind=kOutput, calls=%fused_computation.393 | convolution fusion | flops 6341787648 | bytes 16711680 | tf_op jit(solution)/shard_map/dot_general | solution.py:69
  440.8 13.6 %collective-permute-done.34 = bf16[144,2368]{1,0:T(8,128)(2,1)S(1)} collective-permute-done((bf16[144,2368]{1,0:T(8,128)(2,1)S(1)}, bf16[144,2368]{1,0:T(8,128)(2,1)S(1)}, u32[]{:S(2)}, u32[]{:S(2)}) %collective-permute-start.34) | collective-permute-done | bytes 682016 | tf_op jit(solution)/shard_map/ppermute | solution.py:95
  459.7 9.5 %collective-permute-done.66 = bf16[72,2152]{1,0:T(8,128)(2,1)S(1)} collective-permute-done((bf16[72,2152]{1,0:T(8,128)(2,1)S(1)}, bf16[72,2152]{1,0:T(8,128)(2,1)S(1)}, u32[]{:S(2)}, u32[]{:S(2)}) %collective-permute-start.66) | collective-permute-done | bytes 309920 | tf_op jit(solution)/shard_map/ppermute | solution.py:78
  475.1 12.3 %collective-permute-done.57 = bf16[72,2152]{1,0:T(8,128)(2,1)S(1)} collective-permute-done((bf16[72,2152]{1,0:T(8,128)(2,1)S(1)}, bf16[72,2152]{1,0:T(8,128)(2,1)S(1)}, u32[]{:S(2)}, u32[]{:S(2)}) %collective-permute-start.57) | collective-permute-done | bytes 309920 | tf_op jit(solution)/shard_map/ppermute | solution.py:78
  487.4 8.6 %collective-permute-done.58 = bf16[72,2152]{1,0:T(8,128)(2,1)S(1)} collective-permute-done((bf16[72,2152]{1,0:T(8,128)(2,1)S(1)}, bf16[72,2152]{1,0:T(8,128)(2,1)S(1)}, u32[]{:S(2)}, u32[]{:S(2)}) %collective-permute-start.58) | collective-permute-done | bytes 309920 | tf_op jit(solution)/shard_map/ppermute | solution.py:78
  511.9 9.9 %collective-permute-done.44 = f32[1,4608]{1,0:T(1,128)S(1)} collective-permute-done((f32[1,4608]{1,0:T(1,128)S(1)}, f32[1,4608]{1,0:T(1,128)S(1)}, u32[]{:S(2)}, u32[]{:S(2)}) %collective-permute-start.44) | collective-permute-done | bytes 18464 | tf_op jit(solution)/shard_map/ppermute | solution.py:78
  (446 shorter events, 266.9 us)
Async XLA Ops:
  14.4 61.7 %collective-permute-start.1 = (bf16[384,1152]{1,0:T(8,128)(2,1)S(1)}, bf16[384,1152]{1,0:T(8,128)(2,1)S(1)}, u32[]{:S(2)}, u32[]{:S(2)}) collective-permute-start(bf16[384,1152]{1,0:T(8,128)(2,1)S(1)} %bitcast.59), channel_id=1, source_target_pairs={{0,1},{1,0},{2,3},{3,2},{4,5},{5,4},{6,7},{7,6},{8,9},{9,8},{10,11... | collective-permute-start | bytes 2654216 | tf_op jit(solution)/shard_map/ppermute | solution.py:95
  39.3 34.1 %collective-permute-start.14 = (bf16[72,2728]{1,0:T(8,128)(2,1)S(1)}, bf16[72,2728]{1,0:T(8,128)(2,1)S(1)}, u32[]{:S(2)}, u32[]{:S(2)}) collective-permute-start(bf16[72,2728]{1,0:T(8,128)(2,1)S(1)} %fusion.86), channel_id=1, source_target_pairs={{0,24},{2,26},{4,28},{6,30},{8,16},{10,18},{12,20},{14,22},{16,8},... | collective-permute-start | bytes 1178504 | tf_op jit(solution)/shard_map/ppermute | solution.py:78
  113.9 55.5 %collective-permute-start.15 = (bf16[288,2728]{1,0:T(8,128)(2,1)S(1)}, bf16[288,2728]{1,0:T(8,128)(2,1)}, u32[]{:S(2)}, u32[]{:S(2)}) collective-permute-start(bf16[288,2728]{1,0:T(8,128)(2,1)S(1)} %pad_maximum_fusion.11), channel_id=1, source_target_pairs={{0,4},{2,6},{4,0},{6,2},{8,12},{10,14},{12,8},{14,10},{16,20},{18,... | collective-permute-start | bytes 4713992 | tf_op jit(solution)/shard_map/ppermute | solution.py:78
  114.1 57.3 %collective-permute-start.16 = (bf16[288,2728]{1,0:T(8,128)(2,1)S(1)}, bf16[288,2728]{1,0:T(8,128)(2,1)}, u32[]{:S(2)}, u32[]{:S(2)}) collective-permute-start(bf16[288,2728]{1,0:T(8,128)(2,1)S(1)} %pad_maximum_fusion.11), channel_id=1, source_target_pairs={{0,1},{1,0},{2,3},{3,2},{4,5},{5,4},{6,7},{7,6},{8,9},{9,8},{10,11... | collective-permute-start | bytes 4713992 | tf_op jit(solution)/shard_map/ppermute | solution.py:95
  116.6 44.5 %collective-permute-start.7 = (bf16[144,1792]{1,0:T(8,128)(2,1)S(1)}, bf16[144,1792]{1,0:T(8,128)(2,1)S(1)}, u32[]{:S(2)}, u32[]{:S(2)}) collective-permute-start(bf16[144,1792]{1,0:T(8,128)(2,1)S(1)} %slice.589), channel_id=1, source_target_pairs={{0,1},{1,0},{2,3},{3,2},{4,5},{5,4},{6,7},{7,6},{8,9},{9,8},{10,11... | collective-permute-start | bytes 1548296 | tf_op jit(solution)/shard_map/ppermute | solution.py:95
  116.9 44.2 %collective-permute-start.8 = (bf16[144,1792]{1,0:T(8,128)(2,1)S(1)}, bf16[144,1792]{1,0:T(8,128)(2,1)S(1)}, u32[]{:S(2)}, u32[]{:S(2)}) collective-permute-start(bf16[144,1792]{1,0:T(8,128)(2,1)S(1)} %slice.590), channel_id=1, source_target_pairs={{0,4},{2,6},{4,0},{6,2},{8,12},{10,14},{12,8},{14,10},{16,20},{18,... | collective-permute-start | bytes 1548296 | tf_op jit(solution)/shard_map/ppermute | solution.py:78
  193.7 43.1 %collective-permute-start.25 = (bf16[288,2152]{1,0:T(8,128)(2,1)S(1)}, bf16[288,2152]{1,0:T(8,128)(2,1)S(1)}, u32[]{:S(2)}, u32[]{:S(2)}) collective-permute-start(bf16[288,2152]{1,0:T(8,128)(2,1)S(1)} %copy-done.10), channel_id=1, source_target_pairs={{0,4},{2,6},{4,0},{6,2},{8,12},{10,14},{12,8},{14,10},{16,20},{18,... | collective-permute-start | bytes 3718664 | tf_op jit(solution)/shard_map/ppermute | solution.py:78
  194.0 42.9 %collective-permute-start.26 = (bf16[288,2152]{1,0:T(8,128)(2,1)S(1)}, bf16[288,2152]{1,0:T(8,128)(2,1)S(1)}, u32[]{:S(2)}, u32[]{:S(2)}) collective-permute-start(bf16[288,2152]{1,0:T(8,128)(2,1)S(1)} %copy-done.10), channel_id=1, source_target_pairs={{0,1},{1,0},{2,3},{3,2},{4,5},{5,4},{6,7},{7,6},{8,9},{9,8},{10,11... | collective-permute-start | bytes 3718664 | tf_op jit(solution)/shard_map/ppermute | solution.py:95
  309.8 87.8 %collective-permute-start.63 = (bf16[288,2152]{1,0:T(8,128)(2,1)}, bf16[288,2152]{1,0:T(8,128)(2,1)}, u32[]{:S(2)}, u32[]{:S(2)}) collective-permute-start(bf16[288,2152]{1,0:T(8,128)(2,1)} %pad_maximum_fusion.22), channel_id=1, source_target_pairs={{0,1},{1,0},{2,3},{3,2},{4,5},{5,4},{6,7},{7,6},{8,9},{9,8},{10,11... | collective-permute-start | bytes 3718664 | tf_op jit(solution)/shard_map/ppermute | solution.py:95
  312.4 85.2 %collective-permute-start.62 = (bf16[288,2152]{1,0:T(8,128)(2,1)}, bf16[288,2152]{1,0:T(8,128)(2,1)}, u32[]{:S(2)}, u32[]{:S(2)}) collective-permute-start(bf16[288,2152]{1,0:T(8,128)(2,1)} %pad_maximum_fusion.21), channel_id=1, source_target_pairs={{0,4},{2,6},{4,0},{6,2},{8,12},{10,14},{12,8},{14,10},{16,20},{18,... | collective-permute-start | bytes 3718664 | tf_op jit(solution)/shard_map/ppermute | solution.py:78
  317.4 53.2 %collective-permute-start.30 = (bf16[384,1152]{1,0:T(8,128)(2,1)}, bf16[384,1152]{1,0:T(8,128)(2,1)}, u32[]{:S(2)}, u32[]{:S(2)}) collective-permute-start(bf16[384,1152]{1,0:T(8,128)(2,1)} %convert_element_type.277), channel_id=1, source_target_pairs={{0,2},{2,0},{4,6},{6,4},{8,10},{10,8},{12,14},{14,12},{16,18},{18,... | collective-permute-start | bytes 2654216 | tf_op jit(solution)/shard_map/ppermute | solution.py:78
  350.9 86.2 %collective-permute-start.55 = (bf16[288,2152]{1,0:T(8,128)(2,1)}, bf16[288,2152]{1,0:T(8,128)(2,1)}, u32[]{:S(2)}, u32[]{:S(2)}) collective-permute-start(bf16[288,2152]{1,0:T(8,128)(2,1)} %pad_maximum_fusion.20), channel_id=1, source_target_pairs={{0,1},{1,0},{2,3},{3,2},{4,5},{5,4},{6,7},{7,6},{8,9},{9,8},{10,11... | collective-permute-start | bytes 3718664 | tf_op jit(solution)/shard_map/ppermute | solution.py:95
  365.5 72.7 %collective-permute-start.54 = (bf16[288,2152]{1,0:T(8,128)(2,1)}, bf16[288,2152]{1,0:T(8,128)(2,1)}, u32[]{:S(2)}, u32[]{:S(2)}) collective-permute-start(bf16[288,2152]{1,0:T(8,128)(2,1)} %pad_maximum_fusion.19), channel_id=1, source_target_pairs={{0,4},{2,6},{4,0},{6,2},{8,12},{10,14},{12,8},{14,10},{16,20},{18,... | collective-permute-start | bytes 3718664 | tf_op jit(solution)/shard_map/ppermute | solution.py:78
  400.0 58.5 %collective-permute-start.64 = (bf16[72,2152]{1,0:T(8,128)(2,1)S(1)}, bf16[72,2152]{1,0:T(8,128)(2,1)S(1)}, u32[]{:S(2)}, u32[]{:S(2)}) collective-permute-start(bf16[72,2152]{1,0:T(8,128)(2,1)S(1)} %get-tuple-element.180), channel_id=1, source_target_pairs={{0,8},{2,10},{4,12},{6,14},{8,0},{10,2},{12,4},{14,6},{16,24},{18,... | collective-permute-start | bytes 929672 | tf_op jit(solution)/shard_map/ppermute | solution.py:78
  400.9 58.1 %collective-permute-start.65 = (bf16[72,2152]{1,0:T(8,128)(2,1)S(1)}, bf16[72,2152]{1,0:T(8,128)(2,1)S(1)}, u32[]{:S(2)}, u32[]{:S(2)}) collective-permute-start(bf16[72,2152]{1,0:T(8,128)(2,1)S(1)} %get-tuple-element.179), channel_id=1, source_target_pairs={{0,16},{2,18},{4,20},{6,22},{8,24},{10,26},{12,28},{14,30},{16,0},... | collective-permute-start | bytes 929672 | tf_op jit(solution)/shard_map/ppermute | solution.py:78
  417.4 39.6 %collective-permute-start.31 = (f32[768,1152]{1,0:T(8,128)S(1)}, f32[768,1152]{1,0:T(8,128)S(1)}, u32[]{:S(2)}, u32[]{:S(2)}) collective-permute-start(f32[768,1152]{1,0:T(8,128)S(1)} %slice.653), channel_id=1, source_target_pairs={{0,2},{2,0},{4,6},{6,4},{8,10},{10,8},{12,14},{14,12},{16,18},{18,... | collective-permute-start | bytes 10616840 | tf_op jit(solution)/shard_map/ppermute | solution.py:78
  458.5 37.5 %collective-permute-start.58 = (bf16[72,2152]{1,0:T(8,128)(2,1)S(1)}, bf16[72,2152]{1,0:T(8,128)(2,1)S(1)}, u32[]{:S(2)}, u32[]{:S(2)}) collective-permute-start(bf16[72,2152]{1,0:T(8,128)(2,1)S(1)} %get-tuple-element.184), channel_id=1, source_target_pairs={{0,24},{2,26},{4,28},{6,30},{8,16},{10,18},{12,20},{14,22},{16,8},... | collective-permute-start | bytes 929672 | tf_op jit(solution)/shard_map/ppermute | solution.py:78
  459.0 43.0 %collective-permute-start.37 = (bf16[288,2368]{1,0:T(8,128)(2,1)S(1)}, bf16[288,2368]{1,0:T(8,128)(2,1)S(1)}, u32[]{:S(2)}, u32[]{:S(2)}) collective-permute-start(bf16[288,2368]{1,0:T(8,128)(2,1)S(1)} %pad_maximum_fusion.16), channel_id=1, source_target_pairs={{0,1},{1,0},{2,3},{3,2},{4,5},{5,4},{6,7},{7,6},{8,9},{9,8},{10,11... | collective-permute-start | bytes 4091912 | tf_op jit(solution)/shard_map/ppermute | solution.py:95
  469.2 32.9 %collective-permute-start.36 = (bf16[288,2368]{1,0:T(8,128)(2,1)S(1)}, bf16[288,2368]{1,0:T(8,128)(2,1)S(1)}, u32[]{:S(2)}, u32[]{:S(2)}) collective-permute-start(bf16[288,2368]{1,0:T(8,128)(2,1)S(1)} %pad_maximum_fusion.15), channel_id=1, source_target_pairs={{0,4},{2,6},{4,0},{6,2},{8,12},{10,14},{12,8},{14,10},{16,20},{18,... | collective-permute-start | bytes 4091912 | tf_op jit(solution)/shard_map/ppermute | solution.py:78
  470.6 66.7 %collective-permute-start.67 = (f32[36,2152]{1,0:T(8,128)}, f32[36,2152]{1,0:T(8,128)}, u32[]{:S(2)}, u32[]{:S(2)}) collective-permute-start(f32[36,2152]{1,0:T(8,128)} %get-tuple-element.197), channel_id=1, source_target_pairs={{0,2},{2,0},{4,6},{6,4},{8,10},{10,8},{12,14},{14,12},{16,18},{18,... | collective-permute-start | bytes 929672 | tf_op jit(solution)/shard_map/ppermute | solution.py:78
  497.1 43.4 %collective-permute-start.59 = (f32[36,2152]{1,0:T(8,128)}, f32[36,2152]{1,0:T(8,128)}, u32[]{:S(2)}, u32[]{:S(2)}) collective-permute-start(f32[36,2152]{1,0:T(8,128)} %get-tuple-element.199), channel_id=1, source_target_pairs={{0,2},{2,0},{4,6},{6,4},{8,10},{10,8},{12,14},{14,12},{16,18},{18,... | collective-permute-start | bytes 929672 | tf_op jit(solution)/shard_map/ppermute | solution.py:78
  505.2 40.9 %collective-permute-start.38 = (bf16[72,2368]{1,0:T(8,128)(2,1)}, bf16[72,2368]{1,0:T(8,128)(2,1)}, u32[]{:S(2)}, u32[]{:S(2)}) collective-permute-start(bf16[72,2368]{1,0:T(8,128)(2,1)} %get-tuple-element.174), channel_id=1, source_target_pairs={{0,8},{2,10},{4,12},{6,14},{8,0},{10,2},{12,4},{14,6},{16,24},{18,... | collective-permute-start | bytes 1022984 | tf_op jit(solution)/shard_map/ppermute | solution.py:78
  505.2 40.9 %collective-permute-start.39 = (bf16[72,2368]{1,0:T(8,128)(2,1)}, bf16[72,2368]{1,0:T(8,128)(2,1)}, u32[]{:S(2)}, u32[]{:S(2)}) collective-permute-start(bf16[72,2368]{1,0:T(8,128)(2,1)} %get-tuple-element.173), channel_id=1, source_target_pairs={{0,16},{2,18},{4,20},{6,22},{8,24},{10,26},{12,28},{14,30},{16,0},... | collective-permute-start | bytes 1022984 | tf_op jit(solution)/shard_map/ppermute | solution.py:78
  540.4 32.1 %collective-permute-start.32 = (f32[384,1152]{1,0:T(8,128)}, f32[384,1152]{1,0:T(8,128)}, u32[]{:S(2)}, u32[]{:S(2)}) collective-permute-start(f32[384,1152]{1,0:T(8,128)} %slice.660), channel_id=1, source_target_pairs={{0,2},{2,0},{4,6},{6,4},{8,10},{10,8},{12,14},{14,12},{16,18},{18,... | collective-permute-start | bytes 5308424 | tf_op jit(solution)/shard_map/ppermute | solution.py:78
  (103 other events, 1289.5 us)
